TPU v7x, 128 devices: a whole 4x4x4 slice. The times are simulated.
128 devices in a mesh: req: 64 (over z, y, x), tp: 2 (over core).
Axes of the slice: x: 4, y: 4, z: 4, core: 2. Of those that a mesh axis runs over, the one named last changes fastest.
Arguments:
- patches: bfloat16 [16384, 1664], P('req', 'tp'), may hold values from -6 to 6
- segment: int32 [16384], P('req'), may hold values from 0 to 2, as said below
- owner: int32 [128], P('req'), may hold values from 0 to 63, as said below
- w_qkv: bfloat16 [3, 1664, 1664], P(None, None, 'tp'), as said below
- w_out: bfloat16 [1664, 1664], P('tp'), may hold values from -0.15625 to 0.15625
- w_up: bfloat16 [1664, 8192], P(None, 'tp'), may hold values from -0.15625 to 0.15625
- w_down: bfloat16 [8192, 1664], P('tp'), may hold values from -0.0625 to 0.0625
- gains: float32 [3, 1664], replicated, may hold values from 0.1 to 1.9
- w_merge: bfloat16 [6656, 4096], P(None, 'tp'), may hold values from -0.078125 to 0.078125
Outputs:
- routed: bfloat16 [4096, 4096], P('req', 'tp')
Inputs may be any that keep to these rules, and one draw needn't show every extreme that they name: On each shard the requests 0 to 1 lie in order from slot 0, request j filling 4 c_j consecutive slots with c_j from 1 to 32 merged rows, one request of every shard exactly 32; the remaining slots are padding with segment 2. `owner`: owners of the requests of one shard are all different; every device owns exactly one request of each index j from 0 to 1 among all shards. `w_qkv`: Real-valued projections of order one in their products, with no further structure promised.
All inputs are finite; a program needn't handle non-finite values.
Results may differ from a plain program's by a relative error of at most 0.018.
Values may be sent and summed in bfloat16 or wider, within the bound.
A program may use at most 192 MiB of HBM per device.

v0:
```python
import jax
import jax.numpy as jnp
from jax import lax
from jax.sharding import PartitionSpec as P

HEAD_DIM = 104
CAP = 32


def norm_rows(values, gain):
    center = values - jnp.mean(values, axis=-1, keepdims=True)
    spread = jnp.mean(center * center, axis=-1, keepdims=True)
    return center * lax.rsqrt(spread + 1e-06) * gain


def attend(query, keys, values, segment):
    count = query.shape[0]
    block = min(512, count)
    scale = HEAD_DIM ** (-0.5)
    scores = jnp.einsum("qhd,khd->hqk", query, keys, preferred_element_type=jnp.float32) * scale
    same = segment[0:block, None] == segment[None, :]
    scores = jnp.where(same[None], scores, -1e30)
    top = jnp.max(scores, axis=-1, keepdims=True)
    expo = jnp.exp(scores - top)
    weights = (expo / jnp.sum(expo, axis=-1, keepdims=True)).astype(jnp.bfloat16)
    context = jnp.einsum(
        "hqk,khd->qhd", weights, values, preferred_element_type=jnp.float32
    ).astype(jnp.bfloat16)
    outputs = context.reshape(block, -1)
    return outputs


def local(patches, segment, owner, w_qkv, w_out, w_up, w_down, gains, w_merge):
    owners_count = lax.axis_size("req")
    rows_full = lax.all_gather(patches, "tp", axis=1, tiled=True)
    count = rows_full.shape[0]
    width = rows_full.shape[1]
    resid = rows_full.astype(jnp.float32)
    normed = norm_rows(resid, gains[0]).astype(jnp.bfloat16)
    packed = jnp.einsum("td,sde->ste", normed, w_qkv, preferred_element_type=jnp.float32).astype(
        jnp.bfloat16
    )
    local_heads = w_qkv.shape[2] // HEAD_DIM
    query = packed[0].reshape(count, local_heads, HEAD_DIM)
    keys = packed[1].reshape(count, local_heads, HEAD_DIM)
    values = packed[2].reshape(count, local_heads, HEAD_DIM)
    context = attend(query, keys, values, segment)
    first = resid + lax.psum(
        jnp.dot(context, w_out, preferred_element_type=jnp.float32).astype(jnp.bfloat16), "tp"
    ).astype(jnp.float32)
    hidden = jax.nn.gelu(
        jnp.dot(
            norm_rows(first, gains[1]).astype(jnp.bfloat16),
            w_up,
            preferred_element_type=jnp.float32,
        ),
        approximate=False,
    ).astype(jnp.bfloat16)
    second = first + lax.psum(
        jnp.dot(hidden, w_down, preferred_element_type=jnp.float32).astype(jnp.bfloat16), "tp"
    ).astype(jnp.float32)
    final = norm_rows(second, gains[2]).astype(jnp.bfloat16).reshape(count // 4, 4 * width)
    projected = jnp.dot(final, w_merge, preferred_element_type=jnp.float32).astype(jnp.bfloat16)
    requests_here = owner.shape[0]
    out_width = projected.shape[1]
    first_seg = segment[::4]
    picks = first_seg[:, None] == jnp.arange(requests_here, dtype=jnp.int32)[None, :]
    looked = jnp.sum(jnp.where(picks, owner[None, :], 0), axis=1)
    dest = jnp.where(first_seg < requests_here, looked, owners_count)
    onehot = (dest[:, None] == jnp.arange(owners_count, dtype=jnp.int32)[None, :]).astype(jnp.int32)
    rank = jnp.sum((jnp.cumsum(onehot, axis=0) - 1) * onehot, axis=1)
    outgoing = jnp.zeros((owners_count, CAP, out_width), jnp.bfloat16)
    outgoing = outgoing.at[dest, rank].set(projected, mode="drop")
    outgoing = outgoing.reshape(owners_count * CAP, out_width)
    marks = owner[None, :] == jnp.arange(owners_count, dtype=jnp.int32)[:, None]
    labels = jnp.sum(
        jnp.where(marks, jnp.arange(1, requests_here + 1, dtype=jnp.int32)[None, :], 0), axis=1
    )
    arrived, arrived_labels = (
        lax.all_to_all(outgoing, "req", split_axis=0, concat_axis=0, tiled=True),
        lax.all_to_all(labels, "req", split_axis=0, concat_axis=0, tiled=True),
    )
    arrived = arrived.reshape(owners_count, CAP * out_width)
    select = (
        arrived_labels[None, :] == jnp.arange(1, requests_here + 1, dtype=jnp.int32)[:, None]
    ).astype(jnp.bfloat16)
    placed = jnp.dot(select, arrived, preferred_element_type=jnp.float32).astype(jnp.bfloat16)
    return placed.reshape(requests_here * CAP, out_width)


def solution(mesh):
    in_specs = (
        P("req", "tp"),
        P("req"),
        P("req"),
        P(None, None, "tp"),
        P("tp", None),
        P(None, "tp"),
        P("tp", None),
        P(),
        P(None, "tp"),
    )
    out_specs = P("req", "tp")
    return jax.shard_map(local, mesh=mesh, in_specs=in_specs, out_specs=out_specs, check_vma=False)
```

profile of v0, /device:TPU:0, one launch (start us, length us, event | category | flops | bytes accessed | tf_op | source)
XLA Modules:
  0.0 305.9 jit_solution(8156219259770671583)
XLA Ops:
  6.5 0.0 copy-start
  6.5 0.0 all-reduce.3.cloned.1.call-start
  6.5 1.0 slice_reduce_fusion.1
  7.5 0.9 broadcast_compare_fusion
  8.4 4.1 %all_gather.3 = bf16[256,1664]{0,1:T(8,128)(2,1)} all-gather(bf16[256,832]{0,1:T(8,128)(2,1)} %param.9), channel_id=1, replica_groups=mesh['req'=64,'tp'=2] {'tp'}, dimensions={1}, use_global_device_ids=true | all-gather | bytes 1277952 | tf_op jit(solution)/shard_map/all_gather | solution.py:35
  12.5 2.2 copy.19
  14.7 1.3 convert_reduce_fusion
  16.1 1.5 fusion.45
  17.6 6.3 %fusion.48 = bf16[3,256,832]{1,2,0:T(8,128)(2,1)S(1)} fusion(bf16[3,1664,832]{1,2,0:T(8,128)(2,1)} %param.12, bf16[256,1664]{1,0:T(8,128)(2,1)} %copy.19, f32[1664]{0:T(1024)S(1)} %get-tuple-element.6, f32[256]{0:T(256)S(1)} %add_rsqrt_fusion.2, f32[256]{0:T(256)S(1)} %broadcast_multiply_fusion.2), kind=kOutput, calls=%fused_computation.73 | convolution fusion | flops 2129281024 | bytes 10445312 | tf_op jit(solution)/shard_map/td,sde->ste/dot_general | solution.py:40
  23.9 1.0 fusion.109
  24.9 3.3 %fusion.110 = (f32[8,256]{1,0:T(8,128)S(1)}, f32[8,256,256]{1,2,0:T(8,128)}) fusion(pred[256,256]{0,1:T(8,128)(4,1)S(1)} %broadcast_compare_fusion, bf16[256,8,104]{0,2,1:T(8,128)(2,1)} %bitcast.41, bf16[256,8,104]{0,2,1:T(8,128)(2,1)} %bitcast.40), kind=kOutput, calls=%fused_computation.152 | convolution fusion | flops 111149312 | bytes 3022848 | tf_op jit(solution)/shard_map/sub | solution.py:24
  28.2 1.9 convolution_convert_fusion.5
  30.1 0.0 copy-start.5
  30.1 0.0 copy-done
  30.1 2.1 convolution_convert_fusion.2
  32.2 0.0 all-reduce.3.cloned.1.call-update
  32.2 0.2 all-reduce.5.cloned.1.call-start
  32.5 0.0 copy-done.5
  32.5 0.2 slice.21
  32.6 27.1 %all-reduce.3.cloned.1.call-done = bf16[256,1664]{1,0:T(8,128)(2,1)} async-done(((bf16[256,1664]{1,0:T(8,128)(2,1)}), bf16[256,1664]{1,0:T(8,128)(2,1)}) %all-reduce.3.cloned.1.call-update) | async-done | bytes 851984 | tf_op jit(solution)/shard_map/psum | solution.py:48
  59.8 1.7 fusion.49
  61.5 1.8 multiply_reduce_fusion.1
  63.3 0.0 copy-start.6
  63.3 0.0 copy-start.2
  63.4 0.0 copy-start.3
  63.4 24.8 %convolution_convert_fusion.1 = bf16[256,1664]{1,0:T(8,128)(2,1)} fusion(bf16[4096,1664]{1,0:T(8,128)(2,1)} %param.15, bf16[1664,4096]{1,0:T(8,128)(2,1)} %param.14, bf16[256,1664]{1,0:T(8,128)(2,1)} %all-reduce.3.cloned.1.call-done, bf16[256,1664]{1,0:T(8,128)(2,1)} %copy.19, f32[1664]{0:T(1024)S(1)} %get-tuple-element.5, f32[256]{0:T(256)S(1)} %add_rsqrt_fusion.1, ...), kind=kOutput, calls=%fused_computation.22 | convolution fusion | flops 7050887168 | bytes 29827584 | tf_op jit(solution)/shard_map/dot_general | solution.py:60
  88.1 0.0 all-reduce.5.cloned.1.call-update
  88.2 0.1 fusion.70
  88.2 0.7 copy.18
  89.0 10.4 %all-to-all-start = ((s32[64,1,1]{2,1,0:T(1,128)}), s32[64,1,1]{2,1,0:T(1,128)S(1)}, u32[]{:S(2)}, u32[]{:S(2)}) async-start(s32[64,1,1]{2,1,0:T(1,128)} %copy.18), calls=%async_computation | async-start | bytes 65536 | tf_op jit(solution)/shard_map/all_to_all | solution.py:81
  99.4 0.1 fusion.68
  99.5 0.1 reduce_window_sum.11
  99.5 0.2 select_reduce_fusion
  99.7 14.8 %all-reduce.5.cloned.1.call-done = bf16[256,1664]{1,0:T(8,128)(2,1)} async-done(((bf16[256,1664]{1,0:T(8,128)(2,1)}), bf16[256,1664]{1,0:T(8,128)(2,1)}) %all-reduce.5.cloned.1.call-update) | async-done | bytes 851984 | tf_op jit(solution)/shard_map/psum | solution.py:59
  114.6 1.6 fusion.65
  116.2 1.7 multiply_reduce_fusion
  117.9 1.4 multiply_convert_fusion
  119.3 1.7 reshape.111
  121.0 11.4 %convolution_convert_fusion.3 = bf16[64,2048]{1,0:T(8,128)(2,1)S(1)} fusion(bf16[64,6656]{1,0:T(8,128)(2,1)S(1)} %reshape.111, bf16[6656,2048]{1,0:T(8,128)(2,1)} %param.17), kind=kOutput, calls=%fused_computation.27 | convolution fusion | flops 1744961536 | bytes 28377088 | tf_op jit(solution)/shard_map/dot_general | solution.py:63
  132.3 4.3 %broadcast_in_dim.38 = bf16[64,32,2048]{2,1,0:T(8,128)(2,1)} broadcast(bf16[]{:T(256)} %constant.44.clone.1), dimensions={} | broadcast | bytes 8388610 | tf_op jit(solution)/shard_map/broadcast_in_dim | solution.py:72
  136.6 12.4 %scatter_fusion = bf16[64,32,2048]{2,1,0:T(8,128)(2,1)} fusion(bf16[64,32,2048]{2,1,0:T(8,128)(2,1)} %broadcast_in_dim.38, s32[64]{0:T(128)S(1)} %fusion.75, bf16[64,2048]{1,0:T(8,128)(2,1)S(1)} %convolution_convert_fusion.3), kind=kCustom, calls=%fused_computation | custom fusion | bytes 786944 | tf_op jit(solution)/shard_map/scatter | solution.py:73
  149.0 0.0 all-to-all-done
  149.0 11.3 %all-to-all-start.1 = ((bf16[64,32,2048]{2,1,0:T(8,128)(2,1)}), bf16[64,32,2048]{2,1,0:T(8,128)(2,1)}, u32[]{:S(2)}, u32[]{:S(2)}) async-start(bf16[64,32,2048]{2,1,0:T(8,128)(2,1)} %scatter_fusion), calls=%async_computation.1 | async-start | bytes 16777216 | tf_op jit(solution)/shard_map/all_to_all | solution.py:80
  160.3 1.2 reduce
  161.6 119.7 %all-to-all-done.1 = bf16[64,32,2048]{2,1,0:T(8,128)(2,1)} async-done(((bf16[64,32,2048]{2,1,0:T(8,128)(2,1)}), bf16[64,32,2048]{2,1,0:T(8,128)(2,1)}, u32[]{:S(2)}, u32[]{:S(2)}) %all-to-all-start.1) | async-done | bytes 8388640 | tf_op jit(solution)/shard_map/all_to_all | solution.py:80
  281.2 12.1 %copy.22 = bf16[8,8,32,2048]{3,1,2,0:T(8,128)(2,1)} copy(bf16[8,8,32,2048]{3,2,1,0:T(8,128)(2,1)} %bitcast.12) | data formatting | bytes 16777216
  293.3 4.8 %convolution_convert_fusion = bf16[2,65536]{1,0:T(2,128)(2,1)S(1)} fusion(bf16[64,65536]{1,0:T(8,128)(2,1)} %bitcast.38, s32[64]{0:T(128)S(1)} %reduce, s32[2]{0:T(128)S(1)} %iota_add_fusion), kind=kOutput, calls=%fused_computation.2 | convolution fusion | flops 16908416 | bytes 8651016 | tf_op jit(solution)/shard_map/dot_general | solution.py:87
  298.1 0.9 reshape.113
  (16 shorter events, 0.1 us)
Async XLA Ops:
  6.5 23.6 %copy-start = (bf16[832,1664]{1,0:T(8,128)(2,1)S(1)}, bf16[832,1664]{1,0:T(8,128)(2,1)}, u32[]{:S(2)}) copy-start(bf16[832,1664]{1,0:T(8,128)(2,1)} %param.13) | copy-start | bytes 8306692
  6.5 53.2 %all-reduce.3.cloned.1.call-start = ((), (), s32[]{:S(2)}) async-start(), calls=%async_computation.2 | async-start | bytes 1703936 | tf_op jit(solution)/shard_map/psum | solution.py:48
  30.1 2.3 copy-start.5
  32.2 82.3 %all-reduce.5.cloned.1.call-start = ((), (), s32[]{:S(2)}) async-start(), calls=%async_computation.3 | async-start | bytes 1703936 | tf_op jit(solution)/shard_map/psum | solution.py:59
  63.3 24.8 %copy-start.6 = (s32[2]{0:T(128)S(1)}, s32[2]{0:T(128)}, u32[]{:S(2)}) copy-start(s32[2]{0:T(128)} %param.11) | copy-start | bytes 28
  63.3 51.2 %copy-start.2 = (bf16[256,1664]{1,0:T(8,128)(2,1)S(1)}, bf16[256,1664]{1,0:T(8,128)(2,1)}, u32[]{:S(2)}) copy-start(bf16[256,1664]{1,0:T(8,128)(2,1)} %copy.19) | copy-start | bytes 2555908
  63.4 51.2 %copy-start.3 = (bf16[256,1664]{1,0:T(8,128)(2,1)S(1)}, bf16[256,1664]{1,0:T(8,128)(2,1)}, u32[]{:S(2)}) copy-start(bf16[256,1664]{1,0:T(8,128)(2,1)} %all-reduce.3.cloned.1.call-done) | copy-start | bytes 2555908
  89.0 60.1 %all-to-all-start = ((s32[64,1,1]{2,1,0:T(1,128)}), s32[64,1,1]{2,1,0:T(1,128)S(1)}, u32[]{:S(2)}, u32[]{:S(2)}) async-start(s32[64,1,1]{2,1,0:T(1,128)} %copy.18), calls=%async_computation | async-start | bytes 65536 | tf_op jit(solution)/shard_map/all_to_all | solution.py:81
  114.5 3.3 %copy-start.4 = (bf16[256,1664]{1,0:T(8,128)(2,1)S(1)}, bf16[256,1664]{1,0:T(8,128)(2,1)}, u32[]{:S(2)}) copy-start(bf16[256,1664]{1,0:T(8,128)(2,1)} %all-reduce.5.cloned.1.call-done) | copy-start | bytes 2555908
  149.0 132.2 %all-to-all-start.1 = ((bf16[64,32,2048]{2,1,0:T(8,128)(2,1)}), bf16[64,32,2048]{2,1,0:T(8,128)(2,1)}, u32[]{:S(2)}, u32[]{:S(2)}) async-start(bf16[64,32,2048]{2,1,0:T(8,128)(2,1)} %scatter_fusion), calls=%async_computation.1 | async-start | bytes 16777216 | tf_op jit(solution)/shard_map/all_to_all | solution.py:80
  293.3 5.7 %copy-start.1 = (bf16[832,1664]{1,0:T(8,128)(2,1)S(1)}, bf16[832,1664]{1,0:T(8,128)(2,1)}, u32[]{:S(2)}) copy-start(bf16[832,1664]{1,0:T(8,128)(2,1)} %param.13) | copy-start | bytes 8306692
Sparse Core Ops, SparseCore 0:
  32.3 27.3 all-reduce.2
  88.3 26.2 all-reduce.4
where the time goes:
time: 312 us; the launch traced here: 306 us
  waiting for transfers between devices  162 us (52%)
  matrix products  54.5 us (17%)
  local copies, waits for them, and re-layouts  36.4 us (12%)
  starting transfers between devices  22 us (7%)
  other arithmetic  13.7 us (4%)
  between operations  13.6 us (4%)
  blocking collectives  4.13 us (1%)
    all_to_all x1, waiting for transfers between devices, local(): lax.all_to_all(outgoing, 'req', split_axis=0, concat_axis=0, tiled=True)  120 us
    psum x1, waiting for transfers between devices, local(): lax.psum(jnp.dot(context, w_out, preferred_element_type=jnp.float32).asty...  27.1 us
    dot_general x1, matrix products, local(): jnp.dot(hidden, w_down, preferred_element_type=jnp.float32)  24.8 us
    psum x1, waiting for transfers between devices, local(): lax.psum(jnp.dot(hidden, w_down, preferred_element_type=jnp.float32).asty...  14.8 us
    scatter x1, local copies, waits for them, and re-layouts, local(): outgoing = outgoing.at[dest, rank].set(projected, mode='drop')  12.4 us
    unnamed x15, local copies, waits for them, and re-layouts  12.1 us
    dot_general x1, matrix products, local(): jnp.dot(final, w_merge, preferred_element_type=jnp.float32)  11.4 us
    all_to_all x1, starting transfers between devices, local(): lax.all_to_all(outgoing, 'req', split_axis=0, concat_axis=0, tiled=True)  11.3 us
  transfers between devices with their start and end apart: 4, of which 3 were waited for; matrix products, arithmetic and copies ran while one was open for 12% of the time, Pallas kernels for 0%

commit v1 on v0

v1 whole, which is shorter than its diff:
```python
import functools

import jax
import jax.numpy as jnp
from jax import lax
from jax.experimental import pallas as pl
from jax.experimental.pallas import tpu as pltpu
from jax.sharding import PartitionSpec as P

HEAD_DIM = 104
CAP = 32
MESH = pl.DeviceIdType.MESH


def norm_rows(values, gain):
    center = values - jnp.mean(values, axis=-1, keepdims=True)
    spread = jnp.mean(center * center, axis=-1, keepdims=True)
    return center * lax.rsqrt(spread + 1e-06) * gain


def attend(query, keys, values, segment):
    count = query.shape[0]
    scale = HEAD_DIM ** (-0.5)
    scores = jnp.einsum("qhd,khd->hqk", query, keys, preferred_element_type=jnp.float32) * scale
    same = segment[:, None] == segment[None, :]
    scores = jnp.where(same[None], scores, -1e30)
    top = jnp.max(scores, axis=-1, keepdims=True)
    expo = jnp.exp(scores - top)
    weights = (expo / jnp.sum(expo, axis=-1, keepdims=True)).astype(jnp.bfloat16)
    context = jnp.einsum(
        "hqk,khd->qhd", weights, values, preferred_element_type=jnp.float32
    ).astype(jnp.bfloat16)
    return context.reshape(count, -1)


def peer_of(me, step):
    x = lax.rem(lax.rem(me, 4) + lax.rem(step, 4) + 2, 4)
    y = lax.rem(lax.rem(me // 4, 4) + lax.rem(step // 4, 4) + 2, 4)
    z = lax.rem(me // 16 + step // 16 + 2, 4)
    return (z * 4 + y) * 4 + x


SELF_STEP = 42


def route_kernel(
    merged_ref, weight_ref, owner_ref, out_ref,
    wbuf, acc, tiles, inbox, sorted_tiles, landed, own_rows, table, inv_v, inv_s,
    w_sems, send_sem1, recv_sem1, send_sem2, recv_sem2, send_semo, recv_semo, inv_sem,
):
    chunks, depth = wbuf.shape[0], wbuf.shape[1]
    me = lax.axis_index("req")

    def weight_copy(k):
        return pltpu.make_async_copy(weight_ref.at[pl.ds(k * depth, depth), :], wbuf.at[k], w_sems.at[k])

    @pl.loop(0, chunks)
    def _(k):
        weight_copy(k).start()

    barrier = pltpu.get_barrier_semaphore()

    @pl.loop(0, 64)
    def _(step):
        @pl.when(step != SELF_STEP)
        def _():
            pl.semaphore_signal(barrier, inc=1, device_id={"req": peer_of(me, step)}, device_id_type=MESH)

    for j in range(2):
        own_rows[j] = jnp.full((1, 128), owner_ref[j], jnp.int32)

    acc[...] = jnp.zeros_like(acc)

    def step_matmul(k):
        weight_copy(k).wait()
        lhs = merged_ref[:, pl.ds(pl.multiple_of(k * depth, depth), depth)]
        acc[...] += jnp.dot(lhs, wbuf[k], preferred_element_type=jnp.float32)

    first = chunks - 3

    @pl.loop(0, first)
    def _(k):
        step_matmul(k)

    pl.semaphore_wait(barrier, 63)

    @pl.loop(0, 64)
    def _(step):
        @pl.when(step != SELF_STEP)
        def _():
            peer = peer_of(me, step)
            pltpu.make_async_remote_copy(
                src_ref=own_rows.at[peer // 32], dst_ref=table.at[me], send_sem=send_semo, recv_sem=recv_semo,
                device_id={"req": peer}, device_id_type=MESH,
            ).start()

    @pl.loop(first, chunks)
    def _(k):
        step_matmul(k)

    for g in range(4):
        for c in range(16):
            tiles[g * 16 + c] = acc[pl.ds(16 * g, 16), pl.ds(128 * c, 128)].astype(jnp.bfloat16)

    @pl.loop(0, 64)
    def _(step):
        @pl.when(step != SELF_STEP)
        def _():
            peer = peer_of(me, step)
            pltpu.make_async_remote_copy(
                src_ref=tiles.at[peer], dst_ref=inbox.at[me], send_sem=send_sem1, recv_sem=recv_sem1,
                device_id={"req": peer}, device_id_type=MESH,
            ).start()

    inbox[me] = tiles[me]
    table[me] = own_rows[me // 32]

    pltpu.make_async_copy(table.at[pl.ds(0, 63)], table.at[pl.ds(0, 63)], recv_semo).wait()
    lanes = lax.broadcasted_iota(jnp.int32, (64, 1, 128), 2)
    sources = lax.broadcasted_iota(jnp.int32, (64, 1, 128), 0)
    inv_v[...] = jnp.max(jnp.where(table[...] == lanes, sources, 0), axis=0)
    to_scalar = pltpu.make_async_copy(inv_v, inv_s, inv_sem)
    to_scalar.start()
    to_scalar.wait()

    pltpu.make_async_copy(inbox.at[pl.ds(0, 63)], inbox.at[pl.ds(0, 63)], recv_sem1).wait()

    @pl.loop(0, 64)
    def _(d):
        sorted_tiles[d] = inbox[inv_s[0, d]]

    @pl.loop(0, 64)
    def _(step):
        @pl.when(step != SELF_STEP)
        def _():
            peer = peer_of(me, step)
            pltpu.make_async_remote_copy(
                src_ref=sorted_tiles.at[peer], dst_ref=landed.at[me], send_sem=send_sem2, recv_sem=recv_sem2,
                device_id={"req": peer}, device_id_type=MESH,
            ).start()

    landed[me] = sorted_tiles[me]
    pltpu.make_async_copy(landed.at[pl.ds(0, 63)], landed.at[pl.ds(0, 63)], recv_sem2).wait()
    for g in range(4):
        for c in range(16):
            out_ref[pl.ds(16 * g, 16), pl.ds(128 * c, 128)] = landed[g * 16 + c]
    pltpu.make_async_copy(table.at[pl.ds(0, 63)], table.at[pl.ds(0, 63)], send_semo).wait()
    pltpu.make_async_copy(tiles.at[pl.ds(0, 63)], tiles.at[pl.ds(0, 63)], send_sem1).wait()
    pltpu.make_async_copy(sorted_tiles.at[pl.ds(0, 63)], sorted_tiles.at[pl.ds(0, 63)], send_sem2).wait()


def route(merged, w_merge, owner):
    rows, depth = merged.shape
    width = w_merge.shape[1]
    chunk = 512
    chunks = depth // chunk
    return pl.pallas_call(
        route_kernel,
        out_shape=jax.ShapeDtypeStruct((rows, width), jnp.bfloat16),
        in_specs=[
            pl.BlockSpec(memory_space=pltpu.VMEM),
            pl.BlockSpec(memory_space=pl.ANY),
            pl.BlockSpec(memory_space=pltpu.SMEM),
        ],
        out_specs=pl.BlockSpec(memory_space=pltpu.VMEM),
        scratch_shapes=[
            pltpu.VMEM((chunks, chunk, width), jnp.bfloat16),
            pltpu.VMEM((rows, width), jnp.float32),
            pltpu.VMEM((64, 16, 128), jnp.bfloat16),
            pltpu.VMEM((64, 16, 128), jnp.bfloat16),
            pltpu.VMEM((64, 16, 128), jnp.bfloat16),
            pltpu.VMEM((64, 16, 128), jnp.bfloat16),
            pltpu.VMEM((2, 1, 128), jnp.int32),
            pltpu.VMEM((64, 1, 128), jnp.int32),
            pltpu.VMEM((1, 128), jnp.int32),
            pltpu.SMEM((1, 128), jnp.int32),
            pltpu.SemaphoreType.DMA((chunks,)),
        ]
        + [pltpu.SemaphoreType.DMA] * 7,
        compiler_params=pltpu.CompilerParams(
            collective_id=1, has_side_effects=True, vmem_limit_bytes=48 * 1024 * 1024
        ),
        name="route",
    )(merged, w_merge, owner)


def local(patches, segment, owner, w_qkv, w_out, w_up, w_down, gains, w_merge):
    rows_full = lax.all_gather(patches, "tp", axis=1, tiled=True)
    count = rows_full.shape[0]
    width = rows_full.shape[1]
    resid = rows_full.astype(jnp.float32)
    normed = norm_rows(resid, gains[0]).astype(jnp.bfloat16)
    packed = jnp.einsum("td,sde->ste", normed, w_qkv, preferred_element_type=jnp.float32).astype(
        jnp.bfloat16
    )
    local_heads = w_qkv.shape[2] // HEAD_DIM
    query = packed[0].reshape(count, local_heads, HEAD_DIM)
    keys = packed[1].reshape(count, local_heads, HEAD_DIM)
    values = packed[2].reshape(count, local_heads, HEAD_DIM)
    context = attend(query, keys, values, segment)
    first = resid + lax.psum(
        jnp.dot(context, w_out, preferred_element_type=jnp.float32).astype(jnp.bfloat16), "tp"
    ).astype(jnp.float32)
    hidden = jax.nn.gelu(
        jnp.dot(
            norm_rows(first, gains[1]).astype(jnp.bfloat16),
            w_up,
            preferred_element_type=jnp.float32,
        ),
        approximate=False,
    ).astype(jnp.bfloat16)
    second = first + lax.psum(
        jnp.dot(hidden, w_down, preferred_element_type=jnp.float32).astype(jnp.bfloat16), "tp"
    ).astype(jnp.float32)
    final = norm_rows(second, gains[2]).astype(jnp.bfloat16)
    first_seg = segment[::4]
    index = jnp.arange(count // 4, dtype=jnp.int32)
    starts = jnp.sum((first_seg[None, :] < jnp.arange(2, dtype=jnp.int32)[:, None]).astype(jnp.int32), axis=1)
    want = (starts[:, None] + jnp.arange(CAP, dtype=jnp.int32)[None, :]).reshape(-1)
    request = jnp.repeat(jnp.arange(2, dtype=jnp.int32), CAP)
    pick = ((want[:, None] == index[None, :]) & (first_seg[None, :] == request[:, None])).astype(jnp.bfloat16)
    merged = jnp.dot(
        pick, final.reshape(count // 4, 4 * width), preferred_element_type=jnp.float32
    ).astype(jnp.bfloat16)
    return route(merged, w_merge, owner)


def solution(mesh):
    in_specs = (
        P("req", "tp"),
        P("req"),
        P("req"),
        P(None, None, "tp"),
        P("tp", None),
        P(None, "tp"),
        P("tp", None),
        P(),
        P(None, "tp"),
    )
    out_specs = P("req", "tp")
    return jax.shard_map(local, mesh=mesh, in_specs=in_specs, out_specs=out_specs, check_vma=False)
```

time: 312 us -> 159 us (0.51); the launches traced: 306 us -> 158 us
  waiting for transfers between devices: 162 us -> 53.2 us
  Pallas kernels: 0 us -> 30.2 us
  local copies, waits for them, and re-layouts: 36.4 us -> 6.89 us
  starting transfers between devices: 22 us -> 0.22 us
  matrix products: 54.5 us -> 38.8 us
    all_to_all x2 -> x0, waiting for transfers between devices: 120 us -> none  [the longest x1 120 us: local(): lax.all_to_all(outgoing, 'req', split_axis=0, concat_axis=0, tiled=True)]
    pallas_call x0 -> x1, Pallas kernels: none -> 30.2 us  [route(): pl.pallas_call(route_kernel, out_shape=jax.ShapeDtypeStruct((rows, width)...]
    all_to_all x2 -> x0, starting transfers between devices: 21.7 us -> none  [the longest x1 11.3 us: local(): lax.all_to_all(outgoing, 'req', split_axis=0, concat_axis=0, tiled=True)]
    dot_general x2 -> x1, matrix products: 16.1 us -> 0.43 us  [local(): jnp.dot(pick, final.reshape(count // 4, 4 * width), preferred_element_typ...]
    scatter x1 -> x0, local copies, waits for them, and re-layouts: 12.4 us -> none  [local(): outgoing = outgoing.at[dest, rank].set(projected, mode='drop')]
    unnamed x15, local copies, waits for them, and re-layouts: 12.1 us -> 0.74 us
    psum x1, waiting for transfers between devices: 14.8 us -> 25.9 us  [local(): lax.psum(jnp.dot(hidden, w_down, preferred_element_type=jnp.float32).asty...]
    broadcast_in_dim x1, local copies, waits for them, and re-layouts: 4.28 us -> 0.01 us  [local(): request = jnp.repeat(jnp.arange(2, dtype=jnp.int32), CAP)]
  transfers between devices with their start and end apart: 4 -> 2, of which waited for: 3 -> 2; matrix products, arithmetic and copies ran while one was open for 12% -> 0% of each run, Pallas kernels for 0% -> 0%
where the time goes in v1:
time: 159 us; the launch traced here: 158 us
  waiting for transfers between devices  53.2 us (33%)
  matrix products  38.8 us (24%)
  Pallas kernels  30.2 us (19%)
  between operations  13.5 us (8%)
  other arithmetic  11.5 us (7%)
  local copies, waits for them, and re-layouts  6.89 us (4%)
  blocking collectives  4.13 us (3%)
    pallas_call x1, Pallas kernels, route(): pl.pallas_call(route_kernel, out_shape=jax.ShapeDtypeStruct((rows, width)...  30.2 us
    psum x1, waiting for transfers between devices, local(): lax.psum(jnp.dot(context, w_out, preferred_element_type=jnp.float32).asty...  27.3 us
    psum x1, waiting for transfers between devices, local(): lax.psum(jnp.dot(hidden, w_down, preferred_element_type=jnp.float32).asty...  25.9 us
    dot_general x1, matrix products, local(): jnp.dot(hidden, w_down, preferred_element_type=jnp.float32)  24.7 us
    dot_general x1, matrix products, local(): jnp.einsum('td,sde->ste', normed, w_qkv, preferred_element_type=jnp.float32)  6.27 us
    reduce_sum x3, other arithmetic, norm_rows(): spread = jnp.mean(center * center, axis=-1, keepdims=True)  5.03 us
    reduce_sum x3, other arithmetic, norm_rows(): center = values - jnp.mean(values, axis=-1, keepdims=True)  4.7 us
    all_gather x1, blocking collectives, local(): rows_full = lax.all_gather(patches, 'tp', axis=1, tiled=True)  4.13 us
  transfers between devices with their start and end apart: 2, of which 2 were waited for; matrix products, arithmetic and copies ran while one was open for 0% of the time, Pallas kernels for 0%

profile of v1, /device:TPU:0, one launch (start us, length us, event | category | flops | bytes accessed | tf_op | source)
XLA Modules:
  0.0 158.5 jit_solution(4537255086964323773)
XLA Ops:
  6.5 0.0 copy-start
  6.5 0.0 all-reduce.3.cloned.1.call-start
  6.5 1.0 slice_reduce_fusion.1
  7.5 4.1 %all_gather.3 = bf16[256,1664]{0,1:T(8,128)(2,1)} all-gather(bf16[256,832]{0,1:T(8,128)(2,1)} %param.9), channel_id=1, replica_groups=mesh['req'=64,'tp'=2] {'tp'}, dimensions={1}, use_global_device_ids=true | all-gather | bytes 1277952 | tf_op jit(solution)/shard_map/all_gather | solution.py:188
  11.7 2.2 %copy.14 = bf16[256,1664]{1,0:T(8,128)(2,1)} copy(bf16[256,1664]{0,1:T(8,128)(2,1)} %all_gather.3) | data formatting | bytes 1703936 | tf_op jit(solution)/shard_map/all_gather | solution.py:188
  13.8 1.3 convert_reduce_fusion
  15.2 1.5 fusion.45
  16.7 0.0 copy-start.6
  16.7 6.3 %fusion.48 = bf16[3,256,832]{1,2,0:T(8,128)(2,1)S(1)} fusion(bf16[3,1664,832]{1,2,0:T(8,128)(2,1)} %param.12, bf16[256,1664]{1,0:T(8,128)(2,1)} %copy.14, f32[1664]{0:T(1024)S(1)} %get-tuple-element.6, f32[256]{0:T(256)S(1)} %add_rsqrt_fusion.2, f32[256]{0:T(256)S(1)} %broadcast_multiply_fusion.2), kind=kOutput, calls=%fused_computation.71 | convolution fusion | flops 2129281024 | bytes 10445312 | tf_op jit(solution)/shard_map/td,sde->ste/dot_general | solution.py:193
  23.0 1.0 fusion.107
  24.0 0.0 copy-done.6
  24.0 0.1 broadcast_compare_fusion
  24.1 3.4 %fusion.108 = (f32[8,256]{1,0:T(8,128)S(1)}, f32[8,256,256]{1,2,0:T(8,128)}) fusion(pred[256,256]{0,1:T(8,128)(4,1)S(1)} %broadcast_compare_fusion, bf16[256,8,104]{0,2,1:T(8,128)(2,1)} %bitcast.22, bf16[256,8,104]{0,2,1:T(8,128)(2,1)} %bitcast.21), kind=kOutput, calls=%fused_computation.139 | convolution fusion | flops 111149312 | bytes 3022848 | tf_op jit(solution)/shard_map/sub | solution.py:28
  27.5 1.9 %convolution_convert_fusion.4 = bf16[8,104,256]{2,1,0:T(8,128)(2,1)S(1)} fusion(bf16[256,8,104]{0,2,1:T(8,128)(2,1)S(1)} %bitcast.20, f32[8,256,256]{1,2,0:T(8,128)} %get-tuple-element.12, f32[8,256]{1,0:T(8,128)S(1)} %get-tuple-element.11), kind=kOutput, calls=%fused_computation.73 | convolution fusion | flops 110313472 | bytes 2957312 | tf_op jit(solution)/shard_map/hqk,khd->qhd/dot_general | solution.py:30
  29.4 0.0 copy-done
  29.4 2.1 %convolution_convert_fusion.2 = bf16[256,1664]{1,0:T(8,128)(2,1)} fusion(bf16[256,832]{0,1:T(8,128)(2,1)S(1)} %bitcast.23, bf16[832,1664]{1,0:T(8,128)(2,1)S(1)} %copy-done), kind=kOutput, calls=%fused_computation.22 | convolution fusion | flops 709263360 | bytes 4046848 | tf_op jit(solution)/shard_map/dot_general | solution.py:202
  31.5 0.0 all-reduce.3.cloned.1.call-update
  31.5 0.2 all-reduce.5.cloned.1.call-start
  31.7 27.3 %all-reduce.3.cloned.1.call-done = bf16[256,1664]{1,0:T(8,128)(2,1)} async-done(((bf16[256,1664]{1,0:T(8,128)(2,1)}), bf16[256,1664]{1,0:T(8,128)(2,1)}) %all-reduce.3.cloned.1.call-update) | async-done | bytes 851984 | tf_op jit(solution)/shard_map/psum | solution.py:201
  59.0 1.7 %fusion.49 = f32[256]{0:T(256)S(1)} fusion(bf16[256,1664]{1,0:T(8,128)(2,1)} %all-reduce.3.cloned.1.call-done, bf16[256,1664]{1,0:T(8,128)(2,1)} %copy.14), kind=kLoop, calls=%fused_computation.72 | loop fusion | flops 1703680 | bytes 1704960 | tf_op jit(solution)/shard_map/reduce_sum | solution.py:16
  60.7 1.8 %multiply_reduce_fusion.1 = f32[256]{0:T(256)S(1)} fusion(bf16[256,1664]{1,0:T(8,128)(2,1)} %all-reduce.3.cloned.1.call-done, bf16[256,1664]{1,0:T(8,128)(2,1)} %copy.14, f32[256]{0:T(256)S(1)} %broadcast_multiply_fusion.1), kind=kLoop, calls=%fused_computation.69 | loop fusion | flops 2555648 | bytes 1705984 | tf_op jit(solution)/shard_map/reduce_sum | solution.py:17
  62.6 0.0 copy-start.3
  62.6 0.0 copy-start.4
  62.6 24.7 %convolution_convert_fusion.1 = bf16[256,1664]{1,0:T(8,128)(2,1)} fusion(bf16[4096,1664]{1,0:T(8,128)(2,1)} %param.15, bf16[1664,4096]{1,0:T(8,128)(2,1)} %param.14, bf16[256,1664]{1,0:T(8,128)(2,1)} %all-reduce.3.cloned.1.call-done, bf16[256,1664]{1,0:T(8,128)(2,1)} %copy.14, f32[1664]{0:T(1024)S(1)} %get-tuple-element.5, f32[256]{0:T(256)S(1)} %add_rsqrt_fusion.1, ...), kind=kOutput, calls=%fused_computation.21 | convolution fusion | flops 7050887168 | bytes 29827584 | tf_op jit(solution)/shard_map/dot_general | solution.py:213
  87.4 0.0 all-reduce.5.cloned.1.call-update
  87.4 0.2 slice.21
  87.5 0.1 fusion.74
  87.6 0.1 iota_add_fusion
  87.7 0.1 add.57
  87.8 0.1 eq.49
  87.9 25.9 %all-reduce.5.cloned.1.call-done = bf16[256,1664]{1,0:T(8,128)(2,1)} async-done(((bf16[256,1664]{1,0:T(8,128)(2,1)}), bf16[256,1664]{1,0:T(8,128)(2,1)}) %all-reduce.5.cloned.1.call-update) | async-done | bytes 851984 | tf_op jit(solution)/shard_map/psum | solution.py:212
  113.8 0.0 copy-done.3
  113.8 0.0 copy-done.4
  113.8 0.0 copy-start.5
  113.8 1.6 %fusion.65 = f32[256]{0:T(256)S(1)} fusion(bf16[256,1664]{1,0:T(8,128)(2,1)} %all-reduce.5.cloned.1.call-done, bf16[256,1664]{1,0:T(8,128)(2,1)S(1)} %copy-done.4, bf16[256,1664]{1,0:T(8,128)(2,1)S(1)} %copy-done.3), kind=kLoop, calls=%fused_computation.85 | loop fusion | flops 2555648 | bytes 2556928 | tf_op jit(solution)/shard_map/reduce_sum | solution.py:16
  115.5 0.0 copy-start.2
  115.5 1.7 %multiply_reduce_fusion = f32[256]{0:T(256)S(1)} fusion(f32[256]{0:T(256)S(1)} %broadcast_multiply_fusion, bf16[256,1664]{1,0:T(8,128)(2,1)} %all-reduce.5.cloned.1.call-done, bf16[256,1664]{1,0:T(8,128)(2,1)S(1)} %copy-done.4, bf16[256,1664]{1,0:T(8,128)(2,1)S(1)} %copy-done.3), kind=kLoop, calls=%fused_computation.66 | loop fusion | flops 3407616 | bytes 2557952 | tf_op jit(solution)/shard_map/reduce_sum | solution.py:17
  117.2 0.0 copy-done.5
  117.2 1.4 multiply_convert_fusion
  118.6 1.7 %reshape.89 = bf16[64,6656]{1,0:T(8,128)(2,1)S(1)} reshape(bf16[256,1664]{1,0:T(8,128)(2,1)} %multiply_convert_fusion) | data formatting | bytes 1703936 | tf_op jit(solution)/shard_map/reshape | solution.py:223
  120.2 0.4 convolution_convert_fusion.merged_ref
  120.7 0.0 copy-done.2
  120.7 0.0 copy-start.1
  120.7 30.2 %route.1 = bf16[64,2048]{1,0:T(8,128)(2,1)S(1)} custom-call(bf16[64,6656]{1,0:T(8,128)(2,1)S(1)} %convolution_convert_fusion.merged_ref, bf16[6656,2048]{1,0:T(8,128)(2,1)} %weight_ref.1, s32[2]{0:T(128)S(1)} %copy-done.2), custom_call_target="tpu_custom_call" | custom-call | tf_op jit(solution)/shard_map/route/pallas_call | solution.py:157
  150.9 0.7 copy.20
  151.6 0.0 copy-done.1
  (7 shorter events, 0.0 us)
Async XLA Ops:
  6.5 22.9 %copy-start = (bf16[832,1664]{1,0:T(8,128)(2,1)S(1)}, bf16[832,1664]{1,0:T(8,128)(2,1)}, u32[]{:S(2)}) copy-start(bf16[832,1664]{1,0:T(8,128)(2,1)} %param.13) | copy-start | bytes 8306692
  6.5 52.5 %all-reduce.3.cloned.1.call-start = ((), (), s32[]{:S(2)}) async-start(), calls=%async_computation | async-start | bytes 1703936 | tf_op jit(solution)/shard_map/psum | solution.py:201
  16.7 7.3 %copy-start.6 = (s32[256]{0:T(256)S(1)}, s32[256]{0:T(256)}, u32[]{:S(2)}) copy-start(s32[256]{0:T(256)} %param.10) | copy-start | bytes 3076
  31.5 82.3 %all-reduce.5.cloned.1.call-start = ((), (), s32[]{:S(2)}) async-start(), calls=%async_computation.1 | async-start | bytes 1703936 | tf_op jit(solution)/shard_map/psum | solution.py:212
  62.6 51.2 %copy-start.3 = (bf16[256,1664]{1,0:T(8,128)(2,1)S(1)}, bf16[256,1664]{1,0:T(8,128)(2,1)}, u32[]{:S(2)}) copy-start(bf16[256,1664]{1,0:T(8,128)(2,1)} %copy.14) | copy-start | bytes 2555908
  62.6 51.2 %copy-start.4 = (bf16[256,1664]{1,0:T(8,128)(2,1)S(1)}, bf16[256,1664]{1,0:T(8,128)(2,1)}, u32[]{:S(2)}) copy-start(bf16[256,1664]{1,0:T(8,128)(2,1)} %all-reduce.3.cloned.1.call-done) | copy-start | bytes 2555908
  113.8 3.4 %copy-start.5 = (bf16[256,1664]{1,0:T(8,128)(2,1)S(1)}, bf16[256,1664]{1,0:T(8,128)(2,1)}, u32[]{:S(2)}) copy-start(bf16[256,1664]{1,0:T(8,128)(2,1)} %all-reduce.5.cloned.1.call-done) | copy-start | bytes 2555908
  115.5 5.2 %copy-start.2 = (s32[2]{0:T(128)S(1)}, s32[2]{0:T(128)}, u32[]{:S(2)}) copy-start(s32[2]{0:T(128)} %owner_ref.1) | copy-start | bytes 28
  120.7 30.9 %copy-start.1 = (bf16[832,1664]{1,0:T(8,128)(2,1)S(1)}, bf16[832,1664]{1,0:T(8,128)(2,1)}, u32[]{:S(2)}) copy-start(bf16[832,1664]{1,0:T(8,128)(2,1)} %param.13) | copy-start | bytes 8306692
Sparse Core Ops, SparseCore 0:
  31.6 27.3 all-reduce.2
  87.5 26.2 all-reduce.4

commit v2 on v1

--- a/solution.py
+++ b/solution.py
@@ -10,27 +10,6 @@
 HEAD_DIM = 104
 CAP = 32
 MESH = pl.DeviceIdType.MESH
-
-
-def norm_rows(values, gain):
-    center = values - jnp.mean(values, axis=-1, keepdims=True)
-    spread = jnp.mean(center * center, axis=-1, keepdims=True)
-    return center * lax.rsqrt(spread + 1e-06) * gain
-
-
-def attend(query, keys, values, segment):
-    count = query.shape[0]
-    scale = HEAD_DIM ** (-0.5)
-    scores = jnp.einsum("qhd,khd->hqk", query, keys, preferred_element_type=jnp.float32) * scale
-    same = segment[:, None] == segment[None, :]
-    scores = jnp.where(same[None], scores, -1e30)
-    top = jnp.max(scores, axis=-1, keepdims=True)
-    expo = jnp.exp(scores - top)
-    weights = (expo / jnp.sum(expo, axis=-1, keepdims=True)).astype(jnp.bfloat16)
-    context = jnp.einsum(
-        "hqk,khd->qhd", weights, values, preferred_element_type=jnp.float32
-    ).astype(jnp.bfloat16)
-    return context.reshape(count, -1)
 
 
 def peer_of(me, step):
@@ -184,44 +163,240 @@
     )(merged, w_merge, owner)
 
 
+def encode_kernel(
+    patches_ref, segment_ref, qkv_ref, wout_ref, up_ref, down_ref, gains_ref, merged_ref,
+    x_t, qkv_buf, wout_buf, up_buf, down_buf, normed_t, heads, context, resid, acc, normed,
+    pre_a, pre_b, hid_a, hid_b, sent1, got1, sent2, got2,
+    x_sem, qkv_sems, wout_sems, up_sems, down_sems, xs_sem, xr_sem, s1_sems, r1_sems, s2_sems, r2_sems,
+):
+    f32, bf16 = jnp.float32, jnp.bfloat16
+    tp = lax.axis_index("tp")
+    partner = {"tp": 1 - tp}
+    half = patches_ref.shape[0]
+    count = patches_ref.shape[1]
+    width = 2 * half
+    head_count = half // HEAD_DIM
+    hidden_chunk = up_buf.shape[2]
+    hidden_chunks = up_buf.shape[0]
+    cuts = [(0, 512), (512, 512), (1024, 640)]
+
+    def x_copy():
+        return pltpu.make_async_copy(patches_ref, x_t.at[pl.ds(tp * half, half), :], x_sem)
+
+    def qkv_copy(s):
+        return pltpu.make_async_copy(qkv_ref.at[s], qkv_buf.at[s], qkv_sems.at[s])
+
+    def wout_copy(h):
+        return pltpu.make_async_copy(
+            wout_ref.at[pl.ds(HEAD_DIM * h, HEAD_DIM), :], wout_buf.at[pl.ds(128 * h, HEAD_DIM), :], wout_sems.at[h]
+        )
+
+    def up_copy(c):
+        return pltpu.make_async_copy(
+            up_ref.at[:, pl.ds(hidden_chunk * c, hidden_chunk)], up_buf.at[c], up_sems.at[c]
+        )
+
+    def down_copy(c):
+        return pltpu.make_async_copy(
+            down_ref.at[pl.ds(hidden_chunk * c, hidden_chunk), :], down_buf.at[c], down_sems.at[c]
+        )
+
+    def remote(src, dst, send, recv):
+        return pltpu.make_async_remote_copy(
+            src_ref=src, dst_ref=dst, send_sem=send, recv_sem=recv, device_id=partner, device_id_type=MESH
+        )
+
+    x_copy().start()
+    for s in range(3):
+        qkv_copy(s).start()
+
+    barrier = pltpu.get_barrier_semaphore()
+    pl.semaphore_signal(barrier, inc=1, device_id=partner, device_id_type=MESH)
+    pl.semaphore_wait(barrier, 1)
+    x_swap = remote(patches_ref, x_t.at[pl.ds(tp * half, half), :], xs_sem, xr_sem)
+    x_swap.start()
+
+    for h in range(head_count):
+        wout_buf[pl.ds(128 * h + HEAD_DIM, 128 - HEAD_DIM), :] = jnp.zeros((128 - HEAD_DIM, width), bf16)
+        for s in range(3):
+            heads[s, h, pl.ds(HEAD_DIM, 128 - HEAD_DIM), :] = jnp.zeros((128 - HEAD_DIM, count), bf16)
+    seg_rows = jnp.broadcast_to(segment_ref[...], (count, count))
+    same = seg_rows == seg_rows.T
+
+    x_copy().wait()
+    x_swap.wait()
+
+    total = jnp.zeros((1, count), f32)
+    for b in range(width // 128):
+        total += jnp.sum(x_t[pl.ds(128 * b, 128), :].astype(f32), axis=0, keepdims=True)
+    mean = total * (1.0 / width)
+    total = jnp.zeros((1, count), f32)
+    for b in range(width // 128):
+        center = x_t[pl.ds(128 * b, 128), :].astype(f32) - mean
+        total += jnp.sum(center * center, axis=0, keepdims=True)
+    scale = lax.rsqrt(total * (1.0 / width) + 1e-06)
+    for b in range(width // 128):
+        gain = jnp.broadcast_to(gains_ref[0:1, pl.ds(128 * b, 128)], (128, 128)).T
+        gain = jnp.concatenate([gain] * (count // 128), axis=1)
+        x = x_t[pl.ds(128 * b, 128), :].astype(f32)
+        normed_t[pl.ds(128 * b, 128), :] = ((x - mean) * scale * gain).astype(bf16)
+        resid[:, pl.ds(128 * b, 128)] = x.T
+
+    for s in range(3):
+        qkv_copy(s).wait()
+        if s == 0:
+            for h in range(head_count):
+                wout_copy(h).start()
+        for c in range(s * 3, min(s * 3 + 3, hidden_chunks)):
+            up_copy(c).start()
+            down_copy(c).start()
+        product = jnp.dot(qkv_buf[s], normed_t[...], preferred_element_type=f32)
+        for h in range(head_count):
+            heads[s, h, pl.ds(0, HEAD_DIM), :] = product[HEAD_DIM * h : HEAD_DIM * (h + 1)].astype(bf16)
+
+    for h in range(head_count):
+        scores = lax.dot_general(
+            heads[1, h], heads[0, h], (((0,), (0,)), ((), ())), preferred_element_type=f32
+        )
+        scores = jnp.where(same, scores * HEAD_DIM ** (-0.5), -1e30)
+        top = jnp.max(scores, axis=0, keepdims=True)
+        expo = jnp.exp(scores - top)
+        share = 1.0 / jnp.sum(expo, axis=0, keepdims=True)
+        mixed = jnp.dot(heads[2, h], expo.astype(bf16), preferred_element_type=f32) * share
+        context[:, pl.ds(128 * h, 128)] = mixed.T.astype(bf16)
+
+    for h in range(head_count):
+        wout_copy(h).wait()
+    swaps = []
+    for k, (start, size) in enumerate(cuts):
+        cols = pl.ds(start, size)
+        product = jnp.dot(context[...], wout_buf[:, cols], preferred_element_type=f32)
+        sent1[:, cols] = product.astype(bf16)
+        swap = remote(sent1.at[:, cols], got1.at[:, cols], s1_sems.at[k], r1_sems.at[k])
+        swap.start()
+        swaps.append(swap)
+        resid[:, cols] += product
+
+    for swap in swaps:
+        swap.wait()
+
+    def norm_to(which, out, extra):
+        for b in range(count // 32):
+            rows = pl.ds(32 * b, 32)
+            x = resid[rows, :] + extra[rows, :].astype(f32)
+            resid[rows, :] = x
+            center = x - jnp.sum(x, axis=1, keepdims=True) * (1.0 / width)
+            spread = jnp.sum(center * center, axis=1, keepdims=True) * (1.0 / width)
+            out[rows, :] = (center * lax.rsqrt(spread + 1e-06) * gains_ref[which : which + 1, :]).astype(bf16)
+
+    norm_to(1, normed, got1)
+
+    def up(c, out):
+        up_copy(c).wait()
+        out[...] = jnp.dot(normed[...], up_buf[c], preferred_element_type=f32)
+
+    def gelu(pre, out):
+        u = pre[...]
+        out[...] = (0.5 * u * (1.0 + lax.erf(u * 0.5**0.5))).astype(bf16)
+
+    def down(c, hid):
+        down_copy(c).wait()
+        acc[...] += jnp.dot(hid[...], down_buf[c], preferred_element_type=f32)
+
+    acc[...] = jnp.zeros_like(acc)
+    up(0, pre_a)
+    up(1, pre_b)
+    gelu(pre_a, hid_a)
+
+    @pl.loop(0, hidden_chunks // 2 - 1)
+    def _(i):
+        c = 2 * i
+        up(c + 2, pre_a)
+        gelu(pre_b, hid_b)
+        down(c, hid_a)
+        up(c + 3, pre_b)
+        gelu(pre_a, hid_a)
+        down(c + 1, hid_b)
+
+    gelu(pre_b, hid_b)
+    down(hidden_chunks - 2, hid_a)
+    down_copy(hidden_chunks - 1).wait()
+    swaps = []
+    for k, (start, size) in enumerate(cuts):
+        cols = pl.ds(start, size)
+        product = acc[:, cols] + jnp.dot(
+            hid_b[...], down_buf[hidden_chunks - 1, :, cols], preferred_element_type=f32
+        )
+        sent2[:, cols] = product.astype(bf16)
+        swap = remote(sent2.at[:, cols], got2.at[:, cols], s2_sems.at[k], r2_sems.at[k])
+        swap.start()
+        swaps.append(swap)
+        resid[:, cols] += product
+
+    row = lax.broadcasted_iota(jnp.int32, (count, count), 0)
+    token = lax.broadcasted_iota(jnp.int32, (count, count), 1)
+    quarter = count // 4
+    part, request, rank = row // quarter, lax.rem(row, quarter) // CAP, lax.rem(row, CAP)
+    first = jnp.sum((segment_ref[...] < 1).astype(jnp.int32), axis=1, keepdims=True)
+    want = request * first + 4 * rank + part
+    pick = jnp.where((token == want) & (segment_ref[...] == request), 1.0, 0.0).astype(bf16)
+
+    for swap in swaps:
+        swap.wait()
+    norm_to(2, normed, got2)
+    for i in range(4):
+        merged_ref[:, pl.ds(width * i, width)] = jnp.dot(
+            pick[quarter * i : quarter * (i + 1)], normed[...], preferred_element_type=f32
+        ).astype(bf16)
+
+
+def encode(patches_t, segment, qkv_t, w_out, w_up, w_down, gains):
+    half, count = patches_t.shape
+    width = 2 * half
+    hidden = w_up.shape[1]
+    chunk = 512
+    chunks = hidden // chunk
+    heads = half // HEAD_DIM
+    f32, bf16 = jnp.float32, jnp.bfloat16
+    vmem = pl.BlockSpec(memory_space=pltpu.VMEM)
+    anywhere = pl.BlockSpec(memory_space=pl.ANY)
+    dma = pltpu.SemaphoreType.DMA
+    return pl.pallas_call(
+        encode_kernel,
+        out_shape=jax.ShapeDtypeStruct((count // 4, 4 * width), bf16),
+        in_specs=[anywhere, vmem, anywhere, anywhere, anywhere, anywhere, vmem],
+        out_specs=vmem,
+        scratch_shapes=[
+            pltpu.VMEM((width, count), bf16),
+            pltpu.VMEM((3, half, width), bf16),
+            pltpu.VMEM((heads * 128, width), bf16),
+            pltpu.VMEM((chunks, width, chunk), bf16),
+            pltpu.VMEM((chunks, chunk, width), bf16),
+            pltpu.VMEM((width, count), bf16),
+            pltpu.VMEM((3, heads, 128, count), bf16),
+            pltpu.VMEM((count, heads * 128), bf16),
+            pltpu.VMEM((count, width), f32),
+            pltpu.VMEM((count, width), f32),
+            pltpu.VMEM((count, width), bf16),
+            pltpu.VMEM((count, chunk), f32),
+            pltpu.VMEM((count, chunk), f32),
+            pltpu.VMEM((count, chunk), bf16),
+            pltpu.VMEM((count, chunk), bf16),
+        ]
+        + [pltpu.VMEM((count, width), bf16)] * 4
+        + [dma, dma((3,)), dma((heads,)), dma((chunks,)), dma((chunks,)), dma, dma]
+        + [dma((3,))] * 4,
+        compiler_params=pltpu.CompilerParams(
+            collective_id=2, has_side_effects=True, vmem_limit_bytes=60 * 1024 * 1024
+        ),
+        name="encode",
+    )(patches_t, segment, qkv_t, w_out, w_up, w_down, gains)
+
+
 def local(patches, segment, owner, w_qkv, w_out, w_up, w_down, gains, w_merge):
-    rows_full = lax.all_gather(patches, "tp", axis=1, tiled=True)
-    count = rows_full.shape[0]
-    width = rows_full.shape[1]
-    resid = rows_full.astype(jnp.float32)
-    normed = norm_rows(resid, gains[0]).astype(jnp.bfloat16)
-    packed = jnp.einsum("td,sde->ste", normed, w_qkv, preferred_element_type=jnp.float32).astype(
-        jnp.bfloat16
+    merged = encode(
+        patches.T, segment.reshape(1, -1), w_qkv.transpose(0, 2, 1), w_out, w_up, w_down, gains
     )
-    local_heads = w_qkv.shape[2] // HEAD_DIM
-    query = packed[0].reshape(count, local_heads, HEAD_DIM)
-    keys = packed[1].reshape(count, local_heads, HEAD_DIM)
-    values = packed[2].reshape(count, local_heads, HEAD_DIM)
-    context = attend(query, keys, values, segment)
-    first = resid + lax.psum(
-        jnp.dot(context, w_out, preferred_element_type=jnp.float32).astype(jnp.bfloat16), "tp"
-    ).astype(jnp.float32)
-    hidden = jax.nn.gelu(
-        jnp.dot(
-            norm_rows(first, gains[1]).astype(jnp.bfloat16),
-            w_up,
-            preferred_element_type=jnp.float32,
-        ),
-        approximate=False,
-    ).astype(jnp.bfloat16)
-    second = first + lax.psum(
-        jnp.dot(hidden, w_down, preferred_element_type=jnp.float32).astype(jnp.bfloat16), "tp"
-    ).astype(jnp.float32)
-    final = norm_rows(second, gains[2]).astype(jnp.bfloat16)
-    first_seg = segment[::4]
-    index = jnp.arange(count // 4, dtype=jnp.int32)
-    starts = jnp.sum((first_seg[None, :] < jnp.arange(2, dtype=jnp.int32)[:, None]).astype(jnp.int32), axis=1)
-    want = (starts[:, None] + jnp.arange(CAP, dtype=jnp.int32)[None, :]).reshape(-1)
-    request = jnp.repeat(jnp.arange(2, dtype=jnp.int32), CAP)
-    pick = ((want[:, None] == index[None, :]) & (first_seg[None, :] == request[:, None])).astype(jnp.bfloat16)
-    merged = jnp.dot(
-        pick, final.reshape(count // 4, 4 * width), preferred_element_type=jnp.float32
-    ).astype(jnp.bfloat16)
     return route(merged, w_merge, owner)
 
 

time: 159 us -> 63.5 us (0.40)
  waiting for transfers between devices: 53.2 us -> 0 us
  matrix products: 38.8 us -> 0 us
  Pallas kernels: 30.2 us -> 61.4 us
  between operations: 13.5 us -> 0.03 us
  other arithmetic: 11.5 us -> 0 us
  local copies, waits for them, and re-layouts: 6.89 us -> 1.86 us
  blocking collectives: 4.13 us -> 0 us
    psum x2 -> x0, waiting for transfers between devices: 53.2 us -> none  [the longest x1 27.3 us: local(): lax.psum(jnp.dot(context, w_out, preferred_element_type=jnp.float32).asty...]
    dot_general x5 -> x0, matrix products: 35.4 us -> none  [the longest x1 24.7 us: local(): jnp.dot(hidden, w_down, preferred_element_type=jnp.float32)]
    pallas_call x0 -> x1, Pallas kernels: none -> 30.6 us  [encode(): pl.pallas_call(encode_kernel, out_shape=jax.ShapeDtypeStruct((count // 4,...]
    reduce_sum x7 -> x0, other arithmetic: 9.85 us -> none  [the longest x3 5.03 us: norm_rows(): spread = jnp.mean(center * center, axis=-1, keepdims=True)]
    all_gather x1 -> x0, blocking collectives: 4.13 us -> none  [local(): rows_full = lax.all_gather(patches, 'tp', axis=1, tiled=True)]
    sub x1 -> x0, matrix products: 3.35 us -> none  [attend(): expo = jnp.exp(scores - top)]
    all_gather x1 -> x0, local copies, waits for them, and re-layouts: 2.18 us -> none  [local(): rows_full = lax.all_gather(patches, 'tp', axis=1, tiled=True)]
    slice x3 -> x0, local copies, waits for them, and re-layouts: 2.12 us -> none  [the longest x1 0.99 us: local(): keys = packed[1].reshape(count, local_heads, HEAD_DIM)]
  transfers between devices with their start and end apart: 2 -> 0, of which waited for: 2 -> 0; matrix products, arithmetic and copies ran while one was open for 0% -> 0% of each run, Pallas kernels for 0% -> 0%
where the time goes in v2:
time: 63.5 us; the launch traced here: 63.2 us
  Pallas kernels  61.4 us (97%)
  local copies, waits for them, and re-layouts  1.86 us (3%)
    pallas_call x1, Pallas kernels, route(): pl.pallas_call(route_kernel, out_shape=jax.ShapeDtypeStruct((rows, width)...  30.7 us
    pallas_call x1, Pallas kernels, encode(): pl.pallas_call(encode_kernel, out_shape=jax.ShapeDtypeStruct((count // 4,...  30.6 us
    unnamed x5, local copies, waits for them, and re-layouts  1.86 us

profile of v2, /device:TPU:0, one launch (start us, length us, event | category | flops | bytes accessed | tf_op | source)
XLA Modules:
  0.0 63.2 jit_solution(6745378431768149909)
XLA Ops:
  0.0 0.0 copy-start.1
  0.0 30.6 %encode.1.merged_ref = bf16[64,6656]{1,0:T(8,128)(2,1)} custom-call(bf16[832,256]{1,0:T(8,128)(2,1)} %bitcast.4, s32[1,256]{1,0:T(1,128)} %bitcast.5, bf16[3,832,1664]{2,1,0:T(8,128)(2,1)} %bitcast.3, bf16[832,1664]{1,0:T(8,128)(2,1)} %wout_ref.1, bf16[1664,4096]{1,0:T(8,128)(2,1)} %up_ref.1, bf16[4096,1664]{1,0:T(8,128)(2,1)} %down_ref.1, f32[3,1664]{1,0:T(4,128)} %gains_ref.1), custom_call_target="tpu_custom_call" | custom-call | tf_op jit(solution)/shard_map/encode/pallas_call | solution.py:364
  30.6 0.0 copy-done.1
  30.7 0.0 copy-start
  30.7 1.1 %copy-done = bf16[64,6656]{1,0:T(8,128)(2,1)S(1)} copy-done((bf16[64,6656]{1,0:T(8,128)(2,1)S(1)}, bf16[64,6656]{1,0:T(8,128)(2,1)}, u32[]{:S(2)}) %copy-start) | copy-done | bytes 851992
  31.8 30.7 %route.1 = bf16[64,2048]{1,0:T(8,128)(2,1)S(1)} custom-call(bf16[64,6656]{1,0:T(8,128)(2,1)S(1)} %copy-done, bf16[6656,2048]{1,0:T(8,128)(2,1)} %weight_ref.1, s32[2]{0:T(128)S(1)} %copy-done.1), custom_call_target="tpu_custom_call" | custom-call | tf_op jit(solution)/shard_map/route/pallas_call | solution.py:136
  62.5 0.7 %copy.11 = bf16[64,2048]{1,0:T(8,128)(2,1)} copy(bf16[64,2048]{1,0:T(8,128)(2,1)S(1)} %route.1) | data formatting | bytes 524288
Async XLA Ops:
  0.0 30.6 %copy-start.1 = (s32[2]{0:T(128)S(1)}, s32[2]{0:T(128)}, u32[]{:S(2)}) copy-start(s32[2]{0:T(128)} %owner_ref.1) | copy-start | bytes 28
  30.7 1.2 %copy-start = (bf16[64,6656]{1,0:T(8,128)(2,1)S(1)}, bf16[64,6656]{1,0:T(8,128)(2,1)}, u32[]{:S(2)}) copy-start(bf16[64,6656]{1,0:T(8,128)(2,1)} %encode.1.merged_ref) | copy-start | bytes 2555908

commit v3 on v2

v3 whole, which is shorter than its diff:
```python
import functools

import jax
import jax.numpy as jnp
from jax import lax
from jax.experimental import pallas as pl
from jax.experimental.pallas import tpu as pltpu
from jax.sharding import PartitionSpec as P

HEAD_DIM = 104
CAP = 32
MESH = pl.DeviceIdType.MESH


class Place:
    def __init__(self):
        self.me = lax.axis_index("req")
        x, y, z = lax.rem(self.me, 4), lax.rem(self.me // 4, 4), self.me // 16
        self.x = [lax.rem(x + k, 4) for k in range(4)]
        self.y = [lax.rem(y + k, 4) for k in range(4)]
        self.z = [lax.rem(z + k, 4) for k in range(4)]

    def peer(self, dz, dy, dx):
        return self.z[dz] * 16 + self.y[dy] * 4 + self.x[dx]

    def others(self, dys=(2, 3, 1, 0)):
        for dy in dys:
            for dz in (2, 3, 1, 0):
                for dx in (2, 3, 1, 0):
                    if (dz, dy, dx) != (0, 0, 0):
                        yield self.peer(dz, dy, dx)


def swap_kernel(patches_ref, out_ref, x_sem, send_sem, recv_sem):
    tp = lax.axis_index("tp")
    half = patches_ref.shape[0]
    place = out_ref.at[pl.ds(tp * half, half), :]
    mine = pltpu.make_async_copy(patches_ref, place, x_sem)
    mine.start()
    barrier = pltpu.get_barrier_semaphore()
    pl.semaphore_signal(barrier, inc=1, device_id={"tp": 1 - tp}, device_id_type=MESH)
    pl.semaphore_wait(barrier, 1)
    swap = pltpu.make_async_remote_copy(
        src_ref=patches_ref, dst_ref=place, send_sem=send_sem, recv_sem=recv_sem,
        device_id={"tp": 1 - tp}, device_id_type=MESH,
    )
    swap.start()
    mine.wait()
    swap.wait()


def swap_halves(patches_t):
    half, count = patches_t.shape
    dma = pltpu.SemaphoreType.DMA
    return pl.pallas_call(
        swap_kernel,
        out_shape=jax.ShapeDtypeStruct((2 * half, count), patches_t.dtype),
        in_specs=[pl.BlockSpec(memory_space=pl.ANY)],
        out_specs=pl.BlockSpec(memory_space=pltpu.VMEM),
        scratch_shapes=[dma, dma, dma],
        compiler_params=pltpu.CompilerParams(
            collective_id=1, has_side_effects=True, vmem_limit_bytes=62 * 1024 * 1024
        ),
        name="swap_halves",
    )(patches_t)


def layer_kernel(
    x_ref, segment_ref, owner_ref, qkv_ref, wout_ref, up_ref, down_ref, gains_ref, merge_ref, out_ref,
    x_t, qkv_buf, wout_buf, pool, down_buf, normed_t, heads, context, resid, acc, normed,
    pre_a, pre_b, hid_a, hid_b, sent1, got1, sent2, got2,
    merged, tiles, inbox, sorted_tiles, landed, own_rows, table, inv_v, inv_s,
    x_sem, qkv_sems, wout_sems, pool_sems, down_sems, s1_sems, r1_sems, s2_sems, r2_sems,
    send_sem_o, recv_sem_o, inv_sem, send_sem_a, recv_sem_a, send_sem_b, recv_sem_b,
):
    f32, bf16 = jnp.float32, jnp.bfloat16
    tp = lax.axis_index("tp")
    partner = {"tp": 1 - tp}
    place = Place()
    me = place.me
    width, count = x_t.shape
    half = width // 2
    head_count = half // HEAD_DIM
    slots, _, hidden_chunk = pool.shape
    hidden_chunks = down_buf.shape[0]
    out_chunks = merge_ref.shape[1] // hidden_chunk
    cuts = [(0, 512), (512, 512), (1024, 640)]

    def qkv_copy(s):
        return pltpu.make_async_copy(qkv_ref.at[s], qkv_buf.at[s], qkv_sems.at[s])

    def wout_copy(h):
        return pltpu.make_async_copy(
            wout_ref.at[pl.ds(HEAD_DIM * h, HEAD_DIM), :], wout_buf.at[pl.ds(128 * h, HEAD_DIM), :], wout_sems.at[h]
        )

    def up_copy(c):
        return pltpu.make_async_copy(
            up_ref.at[:, pl.ds(hidden_chunk * c, hidden_chunk)], pool.at[c], pool_sems.at[c]
        )

    def merge_cols(m):
        return pl.ds(pl.multiple_of(place.y[(2, 3, 1, 0)[m // 4]] * hidden_chunk, hidden_chunk), hidden_chunk)

    def merge_copy(m):
        slot = (hidden_chunks + m) % slots
        return pltpu.make_async_copy(
            merge_ref.at[pl.ds(width * (m % 4), width), merge_cols(m)], pool.at[slot], pool_sems.at[slot]
        )

    def down_copy(c):
        return pltpu.make_async_copy(
            down_ref.at[pl.ds(hidden_chunk * c, hidden_chunk), :], down_buf.at[c], down_sems.at[c]
        )

    def remote(src, dst, send, recv):
        return pltpu.make_async_remote_copy(
            src_ref=src, dst_ref=dst, send_sem=send, recv_sem=recv, device_id=partner, device_id_type=MESH
        )

    x_copy = pltpu.make_async_copy(x_ref, x_t, x_sem)
    x_copy.start()
    for s in range(3):
        qkv_copy(s).start()

    barrier = pltpu.get_barrier_semaphore()
    for peer in place.others():
        pl.semaphore_signal(barrier, inc=1, device_id={"req": peer}, device_id_type=MESH)
    pl.semaphore_signal(barrier, inc=1, device_id=partner, device_id_type=MESH)

    for j in range(2):
        own_rows[j] = jnp.full((1, 128), owner_ref[j], jnp.int32)
    for h in range(head_count):
        wout_buf[pl.ds(128 * h + HEAD_DIM, 128 - HEAD_DIM), :] = jnp.zeros((128 - HEAD_DIM, width), bf16)
        for s in range(3):
            heads[s, h, pl.ds(HEAD_DIM, 128 - HEAD_DIM), :] = jnp.zeros((128 - HEAD_DIM, count), bf16)
    seg_rows = jnp.broadcast_to(segment_ref[...], (count, count))
    same = seg_rows == seg_rows.T

    x_copy.wait()
    total = jnp.zeros((1, count), f32)
    for b in range(width // 128):
        total += jnp.sum(x_t[pl.ds(128 * b, 128), :].astype(f32), axis=0, keepdims=True)
    mean = total * (1.0 / width)
    total = jnp.zeros((1, count), f32)
    for b in range(width // 128):
        center = x_t[pl.ds(128 * b, 128), :].astype(f32) - mean
        total += jnp.sum(center * center, axis=0, keepdims=True)
    scale = lax.rsqrt(total * (1.0 / width) + 1e-06)
    for b in range(width // 128):
        gain = jnp.broadcast_to(gains_ref[0:1, pl.ds(128 * b, 128)], (128, 128)).T
        gain = jnp.concatenate([gain] * (count // 128), axis=1)
        x = x_t[pl.ds(128 * b, 128), :].astype(f32)
        normed_t[pl.ds(128 * b, 128), :] = ((x - mean) * scale * gain).astype(bf16)
        resid[:, pl.ds(128 * b, 128)] = x.T

    for s in range(3):
        qkv_copy(s).wait()
        if s == 0:
            for h in range(head_count):
                wout_copy(h).start()
        for c in range(s * 3, min(s * 3 + 3, hidden_chunks)):
            up_copy(c).start()
            down_copy(c).start()
        if s == 2:
            for m in range(slots - hidden_chunks):
                merge_copy(m).start()
        product = jnp.dot(qkv_buf[s], normed_t[...], preferred_element_type=f32)
        for h in range(head_count):
            heads[s, h, pl.ds(0, HEAD_DIM), :] = product[HEAD_DIM * h : HEAD_DIM * (h + 1)].astype(bf16)

    for h in range(head_count):
        scores = lax.dot_general(
            heads[1, h], heads[0, h], (((0,), (0,)), ((), ())), preferred_element_type=f32
        )
        scores = jnp.where(same, scores * HEAD_DIM ** (-0.5), -1e30)
        top = jnp.max(scores, axis=0, keepdims=True)
        expo = jnp.exp(scores - top)
        share = 1.0 / jnp.sum(expo, axis=0, keepdims=True)
        mixed = jnp.dot(heads[2, h], expo.astype(bf16), preferred_element_type=f32) * share
        context[:, pl.ds(128 * h, 128)] = mixed.T.astype(bf16)

    for h in range(head_count):
        wout_copy(h).wait()
    pl.semaphore_wait(barrier, 64)
    swaps = []
    for k, (start, size) in enumerate(cuts):
        cols = pl.ds(start, size)
        product = jnp.dot(context[...], wout_buf[:, cols], preferred_element_type=f32)
        sent1[:, cols] = product.astype(bf16)
        swap = remote(sent1.at[:, cols], got1.at[:, cols], s1_sems.at[k], r1_sems.at[k])
        swap.start()
        swaps.append(swap)
        resid[:, cols] += product

    for peer in place.others():
        pltpu.make_async_remote_copy(
            src_ref=own_rows.at[peer // 32], dst_ref=table.at[me], send_sem=send_sem_o, recv_sem=recv_sem_o,
            device_id={"req": peer}, device_id_type=MESH,
        ).start()
    table[me] = own_rows[me // 32]

    for swap in swaps:
        swap.wait()

    def norm_to(which, out, extra):
        for b in range(count // 32):
            rows = pl.ds(32 * b, 32)
            x = resid[rows, :] + extra[rows, :].astype(f32)
            resid[rows, :] = x
            center = x - jnp.sum(x, axis=1, keepdims=True) * (1.0 / width)
            spread = jnp.sum(center * center, axis=1, keepdims=True) * (1.0 / width)
            out[rows, :] = (center * lax.rsqrt(spread + 1e-06) * gains_ref[which : which + 1, :]).astype(bf16)

    norm_to(1, normed, got1)

    def up(c, out):
        up_copy(c).wait()
        out[...] = jnp.dot(normed[...], pool[c], preferred_element_type=f32)

    def gelu(pre, out):
        u = pre[...]
        out[...] = (0.5 * u * (1.0 + lax.erf(u * 0.5**0.5))).astype(bf16)

    def down(c, hid):
        down_copy(c).wait()
        acc[...] += jnp.dot(hid[...], down_buf[c], preferred_element_type=f32)

    acc[...] = jnp.zeros_like(acc)
    up(0, pre_a)
    up(1, pre_b)
    gelu(pre_a, hid_a)
    spare = slots - hidden_chunks
    for m in range(2):
        merge_copy(spare + m).start()

    for c in range(0, hidden_chunks - 2, 2):
        up(c + 2, pre_a)
        gelu(pre_b, hid_b)
        down(c, hid_a)
        merge_copy(spare + c + 2).start()
        up(c + 3, pre_b)
        gelu(pre_a, hid_a)
        down(c + 1, hid_b)
        merge_copy(spare + c + 3).start()

    gelu(pre_b, hid_b)
    down(hidden_chunks - 2, hid_a)
    down_copy(hidden_chunks - 1).wait()
    swaps = []
    for k, (start, size) in enumerate(cuts):
        cols = pl.ds(start, size)
        product = acc[:, cols] + jnp.dot(
            hid_b[...], down_buf[hidden_chunks - 1, :, cols], preferred_element_type=f32
        )
        sent2[:, cols] = product.astype(bf16)
        swap = remote(sent2.at[:, cols], got2.at[:, cols], s2_sems.at[k], r2_sems.at[k])
        swap.start()
        swaps.append(swap)
        resid[:, cols] += product

    row = lax.broadcasted_iota(jnp.int32, (count, count), 0)
    token = lax.broadcasted_iota(jnp.int32, (count, count), 1)
    quarter = count // 4
    part, request, rank = row // quarter, lax.rem(row, quarter) // CAP, lax.rem(row, CAP)
    first = jnp.sum((segment_ref[...] < 1).astype(jnp.int32), axis=1, keepdims=True)
    want = request * first + 4 * rank + part
    pick = jnp.where((token == want) & (segment_ref[...] == request), 1.0, 0.0).astype(bf16)

    def all_but_one(ref):
        return ref.at[pl.ds(0, 63)]

    def wait_all(ref, sem):
        pltpu.make_async_copy(all_but_one(ref), all_but_one(ref), sem).wait()

    wait_all(table, recv_sem_o)
    lanes = lax.broadcasted_iota(jnp.int32, (64, 1, 128), 2)
    sources = lax.broadcasted_iota(jnp.int32, (64, 1, 128), 0)
    inv_v[...] = jnp.max(jnp.where(table[...] == lanes, sources, 0), axis=0)
    to_scalar = pltpu.make_async_copy(inv_v, inv_s, inv_sem)
    to_scalar.start()
    to_scalar.wait()

    for swap in swaps:
        swap.wait()
    norm_to(2, normed, got2)
    for i in range(4):
        merged[:, pl.ds(width * i, width)] = jnp.dot(
            pick[quarter * i : quarter * (i + 1)], normed[...], preferred_element_type=f32
        ).astype(bf16)

    pieces = 4 * out_chunks
    for k, dy in enumerate((2, 3, 1, 0)):
        product = jnp.zeros((quarter, hidden_chunk), f32)
        for i in range(4):
            m = 4 * k + i
            merge_copy(m).wait()
            product += jnp.dot(
                merged[:, pl.ds(width * i, width)], pool[(hidden_chunks + m) % slots], preferred_element_type=f32
            )
            if m + slots < pieces:
                merge_copy(m + slots).start()
        for g in range(4):
            for x in range(4):
                tiles[g * 16 + place.y[dy] * 4 + x] = product[16 * g : 16 * g + 16, 128 * x : 128 * x + 128].astype(bf16)
        for peer in place.others((dy,)):
            pltpu.make_async_remote_copy(
                src_ref=tiles.at[peer], dst_ref=inbox.at[me], send_sem=send_sem_a, recv_sem=recv_sem_a,
                device_id={"req": peer}, device_id_type=MESH,
            ).start()
    inbox[me] = tiles[me]
    wait_all(inbox, recv_sem_a)

    for d in range(64):
        sorted_tiles[d] = inbox[inv_s[0, d]]
    for peer in place.others():
        pltpu.make_async_remote_copy(
            src_ref=sorted_tiles.at[peer], dst_ref=landed.at[me], send_sem=send_sem_b, recv_sem=recv_sem_b,
            device_id={"req": peer}, device_id_type=MESH,
        ).start()
    landed[me] = sorted_tiles[me]
    wait_all(landed, recv_sem_b)
    for g in range(4):
        for c in range(16):
            out_ref[pl.ds(16 * g, 16), pl.ds(128 * c, 128)] = landed[g * 16 + c]
    wait_all(table, send_sem_o)
    wait_all(tiles, send_sem_a)
    wait_all(sorted_tiles, send_sem_b)


def layer(x_t, segment, owner, qkv_t, w_out, w_up, w_down, gains, w_merge):
    width, count = x_t.shape
    half = width // 2
    hidden = w_up.shape[1]
    chunk = 512
    chunks = hidden // chunk
    slots = 12
    heads = half // HEAD_DIM
    rows, out_width = count // 4, w_merge.shape[1]
    f32, bf16 = jnp.float32, jnp.bfloat16
    vmem = pl.BlockSpec(memory_space=pltpu.VMEM)
    smem = pl.BlockSpec(memory_space=pltpu.SMEM)
    anywhere = pl.BlockSpec(memory_space=pl.ANY)
    dma = pltpu.SemaphoreType.DMA
    return pl.pallas_call(
        layer_kernel,
        out_shape=jax.ShapeDtypeStruct((rows, out_width), bf16),
        in_specs=[anywhere, vmem, smem, anywhere, anywhere, anywhere, anywhere, vmem, anywhere],
        out_specs=vmem,
        scratch_shapes=[
            pltpu.VMEM((width, count), bf16),
            pltpu.VMEM((3, half, width), bf16),
            pltpu.VMEM((heads * 128, width), bf16),
            pltpu.VMEM((slots, width, chunk), bf16),
            pltpu.VMEM((chunks, chunk, width), bf16),
            pltpu.VMEM((width, count), bf16),
            pltpu.VMEM((3, heads, 128, count), bf16),
            pltpu.VMEM((count, heads * 128), bf16),
            pltpu.VMEM((count, width), f32),
            pltpu.VMEM((count, width), f32),
            pltpu.VMEM((count, width), bf16),
            pltpu.VMEM((count, chunk), f32),
            pltpu.VMEM((count, chunk), f32),
            pltpu.VMEM((count, chunk), bf16),
            pltpu.VMEM((count, chunk), bf16),
        ]
        + [pltpu.VMEM((count, width), bf16)] * 4
        + [pltpu.VMEM((rows, 4 * width), bf16)]
        + [pltpu.VMEM((64, 16, 128), bf16)] * 4
        + [
            pltpu.VMEM((2, 1, 128), jnp.int32),
            pltpu.VMEM((64, 1, 128), jnp.int32),
            pltpu.VMEM((1, 128), jnp.int32),
            pltpu.SMEM((1, 128), jnp.int32),
        ]
        + [dma, dma((3,)), dma((heads,)), dma((slots,)), dma((chunks,))]
        + [dma((3,))] * 4
        + [dma] * 7,
        compiler_params=pltpu.CompilerParams(
            collective_id=2, has_side_effects=True, vmem_limit_bytes=62 * 1024 * 1024
        ),
        name="layer",
    )(x_t, segment, owner, qkv_t, w_out, w_up, w_down, gains, w_merge)


def local(patches, segment, owner, w_qkv, w_out, w_up, w_down, gains, w_merge):
    x_t = swap_halves(patches.T)
    return layer(
        x_t, segment.reshape(1, -1), owner, w_qkv.transpose(0, 2, 1), w_out, w_up, w_down, gains, w_merge
    )


def solution(mesh):
    in_specs = (
        P("req", "tp"),
        P("req"),
        P("req"),
        P(None, None, "tp"),
        P("tp", None),
        P(None, "tp"),
        P("tp", None),
        P(),
        P(None, "tp"),
    )
    out_specs = P("req", "tp")
    return jax.shard_map(local, mesh=mesh, in_specs=in_specs, out_specs=out_specs, check_vma=False)
```

time: 63.5 us -> 56.4 us (0.89)
  Pallas kernels: 61.4 us -> 54.4 us
    pallas_call x2, Pallas kernels: 61.4 us -> 54.4 us  [the longest x1 51.5 us: layer(): pl.pallas_call(layer_kernel, out_shape=jax.ShapeDtypeStruct((rows, out_wi...]
    unnamed x5 -> x1, local copies, waits for them, and re-layouts: 1.86 us -> 1.67 us
where the time goes in v3:
time: 56.4 us; the launch traced here: 56.1 us
  Pallas kernels  54.4 us (96%)
  local copies, waits for them, and re-layouts  1.67 us (3%)
    pallas_call x1, Pallas kernels, layer(): pl.pallas_call(layer_kernel, out_shape=jax.ShapeDtypeStruct((rows, out_wi...  51.5 us
    pallas_call x1, Pallas kernels, swap_halves(): pl.pallas_call(swap_kernel, out_shape=jax.ShapeDtypeStruct((2 * half, cou...  2.91 us
    unnamed x1, local copies, waits for them, and re-layouts  1.67 us

profile of v3, /device:TPU:0, one launch (start us, length us, event | category | flops | bytes accessed | tf_op | source)
XLA Modules:
  0.0 56.1 jit_solution(16456860932191618714)
XLA Ops:
  0.0 2.9 %swap_halves.1.x_ref = bf16[1664,256]{1,0:T(8,128)(2,1)} custom-call(bf16[832,256]{1,0:T(8,128)(2,1)} %bitcast.4), custom_call_target="tpu_custom_call" | custom-call | tf_op jit(solution)/shard_map/swap_halves/pallas_call | solution.py:55
  2.9 51.5 %layer.1 = bf16[64,2048]{1,0:T(8,128)(2,1)} custom-call(bf16[1664,256]{1,0:T(8,128)(2,1)} %swap_halves.1.x_ref, s32[1,256]{1,0:T(1,128)} %bitcast.5, s32[2]{0:T(128)} %owner_ref.1, bf16[3,832,1664]{2,1,0:T(8,128)(2,1)} %bitcast.3, bf16[832,1664]{1,0:T(8,128)(2,1)} %wout_ref.1, bf16[1664,4096]{1,0:T(8,128)(2,1)} %up_ref.1, bf16[4096,1664]{1,0:T(8,128)(2,1)} %down_ref.1, ...), custom_call_target="tpu_custom_call" | custom-call | tf_op jit(solution)/shard_map/layer/pallas_call | solution.py:345
  54.5 1.7 %copy.11 = bf16[64,2048]{1,0:T(8,128)(2,1)} copy(bf16[64,2048]{1,0:T(8,128)(2,1)} %layer.1) | data formatting | bytes 524288

commit v4 on v3

--- a/solution.py
+++ b/solution.py
@@ -55,7 +55,7 @@
     return pl.pallas_call(
         swap_kernel,
         out_shape=jax.ShapeDtypeStruct((2 * half, count), patches_t.dtype),
-        in_specs=[pl.BlockSpec(memory_space=pl.ANY)],
+        in_specs=[pl.BlockSpec(memory_space=pltpu.HBM)],
         out_specs=pl.BlockSpec(memory_space=pltpu.VMEM),
         scratch_shapes=[dma, dma, dma],
         compiler_params=pltpu.CompilerParams(
@@ -66,11 +66,11 @@
 
 
 def layer_kernel(
-    x_ref, segment_ref, owner_ref, qkv_ref, wout_ref, up_ref, down_ref, gains_ref, merge_ref, out_ref,
-    x_t, qkv_buf, wout_buf, pool, down_buf, normed_t, heads, context, resid, acc, normed,
-    pre_a, pre_b, hid_a, hid_b, sent1, got1, sent2, got2,
+    x_ref, segment_hbm, owner_hbm, qkv_ref, wout_ref, up_ref, down_ref, gains_hbm, merge_ref, out_ref,
+    x_t, segment_ref, owner_ref, gains_ref, qkv_buf, wout_buf, pool, down_buf, normed_t, heads, context, resid, acc, normed,
+    pre_a, pre_b, hid_a, hid_b, sent, got1, got2,
     merged, tiles, inbox, sorted_tiles, landed, own_rows, table, inv_v, inv_s,
-    x_sem, qkv_sems, wout_sems, pool_sems, down_sems, s1_sems, r1_sems, s2_sems, r2_sems,
+    x_sem, small_sems, qkv_sems, wout_sems, pool_sems, down_sems, s1_sems, r1_sems, s2_sems, r2_sems,
     send_sem_o, recv_sem_o, inv_sem, send_sem_a, recv_sem_a, send_sem_b, recv_sem_b,
 ):
     f32, bf16 = jnp.float32, jnp.bfloat16
@@ -119,15 +119,27 @@
         )
 
     x_copy = pltpu.make_async_copy(x_ref, x_t, x_sem)
+    small = [
+        pltpu.make_async_copy(src, dst, small_sems.at[k])
+        for k, (src, dst) in enumerate(
+            ((gains_hbm, gains_ref), (segment_hbm, segment_ref), (owner_hbm, owner_ref))
+        )
+    ]
     x_copy.start()
+    for copy in small:
+        copy.start()
     for s in range(3):
         qkv_copy(s).start()
+    for h in range(head_count):
+        wout_copy(h).start()
 
     barrier = pltpu.get_barrier_semaphore()
     for peer in place.others():
         pl.semaphore_signal(barrier, inc=1, device_id={"req": peer}, device_id_type=MESH)
     pl.semaphore_signal(barrier, inc=1, device_id=partner, device_id_type=MESH)
 
+    for copy in small:
+        copy.wait()
     for j in range(2):
         own_rows[j] = jnp.full((1, 128), owner_ref[j], jnp.int32)
     for h in range(head_count):
@@ -152,13 +164,9 @@
         gain = jnp.concatenate([gain] * (count // 128), axis=1)
         x = x_t[pl.ds(128 * b, 128), :].astype(f32)
         normed_t[pl.ds(128 * b, 128), :] = ((x - mean) * scale * gain).astype(bf16)
-        resid[:, pl.ds(128 * b, 128)] = x.T
 
     for s in range(3):
         qkv_copy(s).wait()
-        if s == 0:
-            for h in range(head_count):
-                wout_copy(h).start()
         for c in range(s * 3, min(s * 3 + 3, hidden_chunks)):
             up_copy(c).start()
             down_copy(c).start()
@@ -187,11 +195,11 @@
     for k, (start, size) in enumerate(cuts):
         cols = pl.ds(start, size)
         product = jnp.dot(context[...], wout_buf[:, cols], preferred_element_type=f32)
-        sent1[:, cols] = product.astype(bf16)
-        swap = remote(sent1.at[:, cols], got1.at[:, cols], s1_sems.at[k], r1_sems.at[k])
+        sent[:, cols] = product.astype(bf16)
+        swap = remote(sent.at[:, cols], got1.at[:, cols], s1_sems.at[k], r1_sems.at[k])
         swap.start()
         swaps.append(swap)
-        resid[:, cols] += product
+        resid[:, cols] = product + x_t[cols, :].astype(f32).T
 
     for peer in place.others():
         pltpu.make_async_remote_copy(
@@ -215,7 +223,6 @@
     norm_to(1, normed, got1)
 
     def up(c, out):
-        up_copy(c).wait()
         out[...] = jnp.dot(normed[...], pool[c], preferred_element_type=f32)
 
     def gelu(pre, out):
@@ -223,38 +230,44 @@
         out[...] = (0.5 * u * (1.0 + lax.erf(u * 0.5**0.5))).astype(bf16)
 
     def down(c, hid):
-        down_copy(c).wait()
         acc[...] += jnp.dot(hid[...], down_buf[c], preferred_element_type=f32)
 
+    def wait_chunks(chunks):
+        for c in chunks:
+            up_copy(c).wait()
+            down_copy(c).wait()
+
     acc[...] = jnp.zeros_like(acc)
+    spare = slots - hidden_chunks
+    middle = hidden_chunks // 2
+    wait_chunks(range(middle))
     up(0, pre_a)
     up(1, pre_b)
     gelu(pre_a, hid_a)
-    spare = slots - hidden_chunks
-    for m in range(2):
-        merge_copy(spare + m).start()
-
     for c in range(0, hidden_chunks - 2, 2):
+        if c + 2 == middle:
+            wait_chunks(range(middle, hidden_chunks))
+            for m in range(middle):
+                merge_copy(spare + m).start()
         up(c + 2, pre_a)
         gelu(pre_b, hid_b)
         down(c, hid_a)
-        merge_copy(spare + c + 2).start()
         up(c + 3, pre_b)
         gelu(pre_a, hid_a)
         down(c + 1, hid_b)
-        merge_copy(spare + c + 3).start()
-
+
+    for m in range(middle, hidden_chunks):
+        merge_copy(spare + m).start()
     gelu(pre_b, hid_b)
     down(hidden_chunks - 2, hid_a)
-    down_copy(hidden_chunks - 1).wait()
     swaps = []
     for k, (start, size) in enumerate(cuts):
         cols = pl.ds(start, size)
         product = acc[:, cols] + jnp.dot(
             hid_b[...], down_buf[hidden_chunks - 1, :, cols], preferred_element_type=f32
         )
-        sent2[:, cols] = product.astype(bf16)
-        swap = remote(sent2.at[:, cols], got2.at[:, cols], s2_sems.at[k], r2_sems.at[k])
+        sent[:, cols] = product.astype(bf16)
+        swap = remote(sent.at[:, cols], got2.at[:, cols], s2_sems.at[k], r2_sems.at[k])
         swap.start()
         swaps.append(swap)
         resid[:, cols] += product
@@ -290,16 +303,21 @@
         ).astype(bf16)
 
     pieces = 4 * out_chunks
+    for m in range(spare + hidden_chunks):
+        merge_copy(m).wait()
     for k, dy in enumerate((2, 3, 1, 0)):
+        for m in range(spare + hidden_chunks, 4 * k + 4):
+            merge_copy(m).wait()
         product = jnp.zeros((quarter, hidden_chunk), f32)
         for i in range(4):
             m = 4 * k + i
-            merge_copy(m).wait()
             product += jnp.dot(
                 merged[:, pl.ds(width * i, width)], pool[(hidden_chunks + m) % slots], preferred_element_type=f32
             )
-            if m + slots < pieces:
-                merge_copy(m + slots).start()
+        for i in range(4):
+            m = 4 * k + i + slots
+            if m < pieces:
+                merge_copy(m).start()
         for g in range(4):
             for x in range(4):
                 tiles[g * 16 + place.y[dy] * 4 + x] = product[16 * g : 16 * g + 16, 128 * x : 128 * x + 128].astype(bf16)
@@ -334,21 +352,23 @@
     hidden = w_up.shape[1]
     chunk = 512
     chunks = hidden // chunk
-    slots = 12
+    slots = 14
     heads = half // HEAD_DIM
     rows, out_width = count // 4, w_merge.shape[1]
     f32, bf16 = jnp.float32, jnp.bfloat16
     vmem = pl.BlockSpec(memory_space=pltpu.VMEM)
-    smem = pl.BlockSpec(memory_space=pltpu.SMEM)
-    anywhere = pl.BlockSpec(memory_space=pl.ANY)
+    hbm = pl.BlockSpec(memory_space=pltpu.HBM)
     dma = pltpu.SemaphoreType.DMA
     return pl.pallas_call(
         layer_kernel,
         out_shape=jax.ShapeDtypeStruct((rows, out_width), bf16),
-        in_specs=[anywhere, vmem, smem, anywhere, anywhere, anywhere, anywhere, vmem, anywhere],
+        in_specs=[hbm] * 9,
         out_specs=vmem,
         scratch_shapes=[
             pltpu.VMEM((width, count), bf16),
+            pltpu.VMEM((1, count), jnp.int32),
+            pltpu.SMEM((2,), jnp.int32),
+            pltpu.VMEM((3, width), f32),
             pltpu.VMEM((3, half, width), bf16),
             pltpu.VMEM((heads * 128, width), bf16),
             pltpu.VMEM((slots, width, chunk), bf16),
@@ -364,7 +384,7 @@
             pltpu.VMEM((count, chunk), bf16),
             pltpu.VMEM((count, chunk), bf16),
         ]
-        + [pltpu.VMEM((count, width), bf16)] * 4
+        + [pltpu.VMEM((count, width), bf16)] * 3
         + [pltpu.VMEM((rows, 4 * width), bf16)]
         + [pltpu.VMEM((64, 16, 128), bf16)] * 4
         + [
@@ -373,7 +393,7 @@
             pltpu.VMEM((1, 128), jnp.int32),
             pltpu.SMEM((1, 128), jnp.int32),
         ]
-        + [dma, dma((3,)), dma((heads,)), dma((slots,)), dma((chunks,))]
+        + [dma, dma((3,)), dma((3,)), dma((heads,)), dma((slots,)), dma((chunks,))]
         + [dma((3,))] * 4
         + [dma] * 7,
         compiler_params=pltpu.CompilerParams(

time: 56.4 us -> 52.9 us (0.938)
  Pallas kernels: 54.4 us -> 51.1 us
    pallas_call x1, Pallas kernels: 51.5 us -> 48.2 us  [layer(): pl.pallas_call(layer_kernel, out_shape=jax.ShapeDtypeStruct((rows, out_wi...]
where the time goes in v4:
time: 52.9 us; the launch traced here: 52.8 us
  Pallas kernels  51.1 us (97%)
  local copies, waits for them, and re-layouts  1.67 us (3%)
    pallas_call x1, Pallas kernels, layer(): pl.pallas_call(layer_kernel, out_shape=jax.ShapeDtypeStruct((rows, out_wi...  48.2 us
    pallas_call x1, Pallas kernels, swap_halves(): pl.pallas_call(swap_kernel, out_shape=jax.ShapeDtypeStruct((2 * half, cou...  2.91 us
    unnamed x1, local copies, waits for them, and re-layouts  1.67 us

profile of v4, /device:TPU:0, one launch (start us, length us, event | category | flops | bytes accessed | tf_op | source)
XLA Modules:
  0.0 52.8 jit_solution(819125751737107677)
XLA Ops:
  0.0 2.9 %swap_halves.1.x_ref = bf16[1664,256]{1,0:T(8,128)(2,1)} custom-call(bf16[832,256]{1,0:T(8,128)(2,1)} %bitcast.4), custom_call_target="tpu_custom_call" | custom-call | tf_op jit(solution)/shard_map/swap_halves/pallas_call | solution.py:55
  2.9 48.2 %layer.1 = bf16[64,2048]{1,0:T(8,128)(2,1)} custom-call(bf16[1664,256]{1,0:T(8,128)(2,1)} %swap_halves.1.x_ref, s32[1,256]{1,0:T(1,128)} %bitcast.5, s32[2]{0:T(128)} %owner_hbm.1, bf16[3,832,1664]{2,1,0:T(8,128)(2,1)} %bitcast.3, bf16[832,1664]{1,0:T(8,128)(2,1)} %wout_ref.1, bf16[1664,4096]{1,0:T(8,128)(2,1)} %up_ref.1, bf16[4096,1664]{1,0:T(8,128)(2,1)} %down_ref.1, ...), custom_call_target="tpu_custom_call" | custom-call | tf_op jit(solution)/shard_map/layer/pallas_call | solution.py:362
  51.1 1.7 %copy.11 = bf16[64,2048]{1,0:T(8,128)(2,1)} copy(bf16[64,2048]{1,0:T(8,128)(2,1)} %layer.1) | data formatting | bytes 524288

commit v5 on v4

--- a/solution.py
+++ b/solution.py
@@ -82,8 +82,9 @@
     half = width // 2
     head_count = half // HEAD_DIM
     slots, _, hidden_chunk = pool.shape
-    hidden_chunks = down_buf.shape[0]
-    out_chunks = merge_ref.shape[1] // hidden_chunk
+    hidden_chunks = down_ref.shape[0] // hidden_chunk
+    middle = hidden_chunks // 2
+    spare = slots - hidden_chunks
     cuts = [(0, 512), (512, 512), (1024, 640)]
 
     def qkv_copy(s):
@@ -108,9 +109,16 @@
             merge_ref.at[pl.ds(width * (m % 4), width), merge_cols(m)], pool.at[slot], pool_sems.at[slot]
         )
 
+    def down_place(c):
+        if c < 3:
+            return down_buf.at[c]
+        if c in (4, 5):
+            return wout_buf.at[pl.ds(hidden_chunk * (c - 4), hidden_chunk), :]
+        return qkv_buf.at[{3: 2, 6: 0, 7: 1}[c], pl.ds(0, hidden_chunk), :]
+
     def down_copy(c):
         return pltpu.make_async_copy(
-            down_ref.at[pl.ds(hidden_chunk * c, hidden_chunk), :], down_buf.at[c], down_sems.at[c]
+            down_ref.at[pl.ds(hidden_chunk * c, hidden_chunk), :], down_place(c), down_sems.at[c]
         )
 
     def remote(src, dst, send, recv):
@@ -167,15 +175,14 @@
 
     for s in range(3):
         qkv_copy(s).wait()
-        for c in range(s * 3, min(s * 3 + 3, hidden_chunks)):
+        for c in range(2 * s, min(2 * s + 2, middle)):
             up_copy(c).start()
-            down_copy(c).start()
-        if s == 2:
-            for m in range(slots - hidden_chunks):
-                merge_copy(m).start()
+            if c < 3:
+                down_copy(c).start()
         product = jnp.dot(qkv_buf[s], normed_t[...], preferred_element_type=f32)
         for h in range(head_count):
             heads[s, h, pl.ds(0, HEAD_DIM), :] = product[HEAD_DIM * h : HEAD_DIM * (h + 1)].astype(bf16)
+    down_copy(3).start()
 
     for h in range(head_count):
         scores = lax.dot_general(
@@ -201,6 +208,10 @@
         swaps.append(swap)
         resid[:, cols] = product + x_t[cols, :].astype(f32).T
 
+    for c in range(middle, hidden_chunks):
+        up_copy(c).start()
+        down_copy(c).start()
+
     for peer in place.others():
         pltpu.make_async_remote_copy(
             src_ref=own_rows.at[peer // 32], dst_ref=table.at[me], send_sem=send_sem_o, recv_sem=recv_sem_o,
@@ -230,7 +241,7 @@
         out[...] = (0.5 * u * (1.0 + lax.erf(u * 0.5**0.5))).astype(bf16)
 
     def down(c, hid):
-        acc[...] += jnp.dot(hid[...], down_buf[c], preferred_element_type=f32)
+        acc[...] += jnp.dot(hid[...], down_place(c)[...], preferred_element_type=f32)
 
     def wait_chunks(chunks):
         for c in chunks:
@@ -238,9 +249,9 @@
             down_copy(c).wait()
 
     acc[...] = jnp.zeros_like(acc)
-    spare = slots - hidden_chunks
-    middle = hidden_chunks // 2
     wait_chunks(range(middle))
+    for m in range(spare):
+        merge_copy(m).start()
     up(0, pre_a)
     up(1, pre_b)
     gelu(pre_a, hid_a)
@@ -256,21 +267,21 @@
         gelu(pre_a, hid_a)
         down(c + 1, hid_b)
 
-    for m in range(middle, hidden_chunks):
-        merge_copy(spare + m).start()
     gelu(pre_b, hid_b)
     down(hidden_chunks - 2, hid_a)
     swaps = []
     for k, (start, size) in enumerate(cuts):
         cols = pl.ds(start, size)
         product = acc[:, cols] + jnp.dot(
-            hid_b[...], down_buf[hidden_chunks - 1, :, cols], preferred_element_type=f32
+            hid_b[...], down_place(hidden_chunks - 1)[:, cols], preferred_element_type=f32
         )
         sent[:, cols] = product.astype(bf16)
         swap = remote(sent.at[:, cols], got2.at[:, cols], s2_sems.at[k], r2_sems.at[k])
         swap.start()
         swaps.append(swap)
         resid[:, cols] += product
+    for m in range(middle, hidden_chunks):
+        merge_copy(spare + m).start()
 
     row = lax.broadcasted_iota(jnp.int32, (count, count), 0)
     token = lax.broadcasted_iota(jnp.int32, (count, count), 1)
@@ -302,22 +313,15 @@
             pick[quarter * i : quarter * (i + 1)], normed[...], preferred_element_type=f32
         ).astype(bf16)
 
-    pieces = 4 * out_chunks
-    for m in range(spare + hidden_chunks):
-        merge_copy(m).wait()
     for k, dy in enumerate((2, 3, 1, 0)):
-        for m in range(spare + hidden_chunks, 4 * k + 4):
-            merge_copy(m).wait()
+        for i in range(4):
+            merge_copy(4 * k + i).wait()
         product = jnp.zeros((quarter, hidden_chunk), f32)
         for i in range(4):
             m = 4 * k + i
             product += jnp.dot(
                 merged[:, pl.ds(width * i, width)], pool[(hidden_chunks + m) % slots], preferred_element_type=f32
             )
-        for i in range(4):
-            m = 4 * k + i + slots
-            if m < pieces:
-                merge_copy(m).start()
         for g in range(4):
             for x in range(4):
                 tiles[g * 16 + place.y[dy] * 4 + x] = product[16 * g : 16 * g + 16, 128 * x : 128 * x + 128].astype(bf16)
@@ -352,7 +356,7 @@
     hidden = w_up.shape[1]
     chunk = 512
     chunks = hidden // chunk
-    slots = 14
+    slots = 16
     heads = half // HEAD_DIM
     rows, out_width = count // 4, w_merge.shape[1]
     f32, bf16 = jnp.float32, jnp.bfloat16
@@ -372,7 +376,7 @@
             pltpu.VMEM((3, half, width), bf16),
             pltpu.VMEM((heads * 128, width), bf16),
             pltpu.VMEM((slots, width, chunk), bf16),
-            pltpu.VMEM((chunks, chunk, width), bf16),
+            pltpu.VMEM((3, chunk, width), bf16),
             pltpu.VMEM((width, count), bf16),
             pltpu.VMEM((3, heads, 128, count), bf16),
             pltpu.VMEM((count, heads * 128), bf16),

time: 52.9 us -> 53 us (level)
  no operation moved by 1% of the time
where the time goes in v5:
time: 53 us; the launch traced here: 52.8 us
  Pallas kernels  51.1 us (96%)
  local copies, waits for them, and re-layouts  1.67 us (3%)
    pallas_call x1, Pallas kernels, layer(): pl.pallas_call(layer_kernel, out_shape=jax.ShapeDtypeStruct((rows, out_wi...  48.2 us
    pallas_call x1, Pallas kernels, swap_halves(): pl.pallas_call(swap_kernel, out_shape=jax.ShapeDtypeStruct((2 * half, cou...  2.91 us
    unnamed x1, local copies, waits for them, and re-layouts  1.67 us

profile of v5, /device:TPU:0, one launch (start us, length us, event | category | flops | bytes accessed | tf_op | source)
XLA Modules:
  0.0 52.8 jit_solution(5381154435373685885)
XLA Ops:
  0.0 2.9 %swap_halves.1.x_ref = bf16[1664,256]{1,0:T(8,128)(2,1)} custom-call(bf16[832,256]{1,0:T(8,128)(2,1)} %bitcast.4), custom_call_target="tpu_custom_call" | custom-call | tf_op jit(solution)/shard_map/swap_halves/pallas_call | solution.py:55
  2.9 48.2 %layer.1 = bf16[64,2048]{1,0:T(8,128)(2,1)} custom-call(bf16[1664,256]{1,0:T(8,128)(2,1)} %swap_halves.1.x_ref, s32[1,256]{1,0:T(1,128)} %bitcast.5, s32[2]{0:T(128)} %owner_hbm.1, bf16[3,832,1664]{2,1,0:T(8,128)(2,1)} %bitcast.3, bf16[832,1664]{1,0:T(8,128)(2,1)} %wout_ref.1, bf16[1664,4096]{1,0:T(8,128)(2,1)} %up_ref.1, bf16[4096,1664]{1,0:T(8,128)(2,1)} %down_ref.1, ...), custom_call_target="tpu_custom_call" | custom-call | tf_op jit(solution)/shard_map/layer/pallas_call | solution.py:366
  51.1 1.7 %copy.11 = bf16[64,2048]{1,0:T(8,128)(2,1)} copy(bf16[64,2048]{1,0:T(8,128)(2,1)} %layer.1) | data formatting | bytes 524288

commit v6 on v5

--- a/solution.py
+++ b/solution.py
@@ -185,15 +185,16 @@
     down_copy(3).start()
 
     for h in range(head_count):
-        scores = lax.dot_general(
-            heads[1, h], heads[0, h], (((0,), (0,)), ((), ())), preferred_element_type=f32
-        )
-        scores = jnp.where(same, scores * HEAD_DIM ** (-0.5), -1e30)
-        top = jnp.max(scores, axis=0, keepdims=True)
-        expo = jnp.exp(scores - top)
-        share = 1.0 / jnp.sum(expo, axis=0, keepdims=True)
-        mixed = jnp.dot(heads[2, h], expo.astype(bf16), preferred_element_type=f32) * share
-        context[:, pl.ds(128 * h, 128)] = mixed.T.astype(bf16)
+        keys = heads[1, h].T
+        for start in range(0, count, 128):
+            queries = pl.ds(start, 128)
+            scores = jnp.dot(keys, heads[0, h, :, queries], preferred_element_type=f32)
+            scores = jnp.where(same[:, start : start + 128], scores * HEAD_DIM ** (-0.5), -1e30)
+            top = jnp.max(scores, axis=0, keepdims=True)
+            expo = jnp.exp(scores - top)
+            share = 1.0 / jnp.sum(expo, axis=0, keepdims=True)
+            mixed = jnp.dot(heads[2, h], expo.astype(bf16), preferred_element_type=f32) * share
+            context[queries, pl.ds(128 * h, 128)] = mixed.T.astype(bf16)
 
     for h in range(head_count):
         wout_copy(h).wait()
@@ -241,14 +242,14 @@
         out[...] = (0.5 * u * (1.0 + lax.erf(u * 0.5**0.5))).astype(bf16)
 
     def down(c, hid):
-        acc[...] += jnp.dot(hid[...], down_place(c)[...], preferred_element_type=f32)
+        product = jnp.dot(hid[...], down_place(c)[...], preferred_element_type=f32)
+        acc[...] = product if c == 0 else acc[...] + product
 
     def wait_chunks(chunks):
         for c in chunks:
             up_copy(c).wait()
             down_copy(c).wait()
 
-    acc[...] = jnp.zeros_like(acc)
     wait_chunks(range(middle))
     for m in range(spare):
         merge_copy(m).start()

time: 53 us -> 54.4 us (1.026)
  Pallas kernels: 51.1 us -> 52.5 us
    pallas_call x1, Pallas kernels: 48.2 us -> 49.6 us  [layer(): pl.pallas_call(layer_kernel, out_shape=jax.ShapeDtypeStruct((rows, out_wi...]
where the time goes in v6:
time: 54.4 us; the launch traced here: 54.2 us
  Pallas kernels  52.5 us (97%)
  local copies, waits for them, and re-layouts  1.67 us (3%)
    pallas_call x1, Pallas kernels, layer(): pl.pallas_call(layer_kernel, out_shape=jax.ShapeDtypeStruct((rows, out_wi...  49.6 us
    pallas_call x1, Pallas kernels, swap_halves(): pl.pallas_call(swap_kernel, out_shape=jax.ShapeDtypeStruct((2 * half, cou...  2.91 us
    unnamed x1, local copies, waits for them, and re-layouts  1.67 us

profile of v6, /device:TPU:0, one launch (start us, length us, event | category | flops | bytes accessed | tf_op | source)
XLA Modules:
  0.0 54.2 jit_solution(17768300892488469998)
XLA Ops:
  0.0 2.9 %swap_halves.1.x_ref = bf16[1664,256]{1,0:T(8,128)(2,1)} custom-call(bf16[832,256]{1,0:T(8,128)(2,1)} %bitcast.4), custom_call_target="tpu_custom_call" | custom-call | tf_op jit(solution)/shard_map/swap_halves/pallas_call | solution.py:55
  2.9 49.6 %layer.1 = bf16[64,2048]{1,0:T(8,128)(2,1)} custom-call(bf16[1664,256]{1,0:T(8,128)(2,1)} %swap_halves.1.x_ref, s32[1,256]{1,0:T(1,128)} %bitcast.5, s32[2]{0:T(128)} %owner_hbm.1, bf16[3,832,1664]{2,1,0:T(8,128)(2,1)} %bitcast.3, bf16[832,1664]{1,0:T(8,128)(2,1)} %wout_ref.1, bf16[1664,4096]{1,0:T(8,128)(2,1)} %up_ref.1, bf16[4096,1664]{1,0:T(8,128)(2,1)} %down_ref.1, ...), custom_call_target="tpu_custom_call" | custom-call | tf_op jit(solution)/shard_map/layer/pallas_call | solution.py:367
  52.5 1.7 %copy.11 = bf16[64,2048]{1,0:T(8,128)(2,1)} copy(bf16[64,2048]{1,0:T(8,128)(2,1)} %layer.1) | data formatting | bytes 524288

commit v7 on v5

--- a/solution.py
+++ b/solution.py
@@ -31,33 +31,28 @@
                         yield self.peer(dz, dy, dx)
 
 
-def swap_kernel(patches_ref, out_ref, x_sem, send_sem, recv_sem):
-    tp = lax.axis_index("tp")
-    half = patches_ref.shape[0]
-    place = out_ref.at[pl.ds(tp * half, half), :]
-    mine = pltpu.make_async_copy(patches_ref, place, x_sem)
-    mine.start()
+def swap_kernel(patches_ref, out_ref, send_sem, recv_sem):
+    partner = {"tp": 1 - lax.axis_index("tp")}
     barrier = pltpu.get_barrier_semaphore()
-    pl.semaphore_signal(barrier, inc=1, device_id={"tp": 1 - tp}, device_id_type=MESH)
+    pl.semaphore_signal(barrier, inc=1, device_id=partner, device_id_type=MESH)
     pl.semaphore_wait(barrier, 1)
     swap = pltpu.make_async_remote_copy(
-        src_ref=patches_ref, dst_ref=place, send_sem=send_sem, recv_sem=recv_sem,
-        device_id={"tp": 1 - tp}, device_id_type=MESH,
+        src_ref=patches_ref, dst_ref=out_ref, send_sem=send_sem, recv_sem=recv_sem,
+        device_id=partner, device_id_type=MESH,
     )
     swap.start()
-    mine.wait()
     swap.wait()
 
 
 def swap_halves(patches_t):
-    half, count = patches_t.shape
     dma = pltpu.SemaphoreType.DMA
+    hbm = pl.BlockSpec(memory_space=pltpu.HBM)
     return pl.pallas_call(
         swap_kernel,
-        out_shape=jax.ShapeDtypeStruct((2 * half, count), patches_t.dtype),
-        in_specs=[pl.BlockSpec(memory_space=pltpu.HBM)],
-        out_specs=pl.BlockSpec(memory_space=pltpu.VMEM),
-        scratch_shapes=[dma, dma, dma],
+        out_shape=jax.ShapeDtypeStruct(patches_t.shape, patches_t.dtype),
+        in_specs=[hbm],
+        out_specs=hbm,
+        scratch_shapes=[dma, dma],
         compiler_params=pltpu.CompilerParams(
             collective_id=1, has_side_effects=True, vmem_limit_bytes=62 * 1024 * 1024
         ),
@@ -66,11 +61,11 @@
 
 
 def layer_kernel(
-    x_ref, segment_hbm, owner_hbm, qkv_ref, wout_ref, up_ref, down_ref, gains_hbm, merge_ref, out_ref,
+    own_ref, other_ref, segment_hbm, owner_hbm, qkv_ref, wout_ref, up_ref, down_ref, gains_hbm, merge_ref, out_ref,
     x_t, segment_ref, owner_ref, gains_ref, qkv_buf, wout_buf, pool, down_buf, normed_t, heads, context, resid, acc, normed,
     pre_a, pre_b, hid_a, hid_b, sent, got1, got2,
     merged, tiles, inbox, sorted_tiles, landed, own_rows, table, inv_v, inv_s,
-    x_sem, small_sems, qkv_sems, wout_sems, pool_sems, down_sems, s1_sems, r1_sems, s2_sems, r2_sems,
+    x_sems, small_sems, qkv_sems, wout_sems, pool_sems, down_sems, s1_sems, r1_sems, s2_sems, r2_sems,
     send_sem_o, recv_sem_o, inv_sem, send_sem_a, recv_sem_a, send_sem_b, recv_sem_b,
 ):
     f32, bf16 = jnp.float32, jnp.bfloat16
@@ -85,7 +80,7 @@
     hidden_chunks = down_ref.shape[0] // hidden_chunk
     middle = hidden_chunks // 2
     spare = slots - hidden_chunks
-    cuts = [(0, 512), (512, 512), (1024, 640)]
+    cuts = [(0, 640), (640, 512), (1152, 512)]
 
     def qkv_copy(s):
         return pltpu.make_async_copy(qkv_ref.at[s], qkv_buf.at[s], qkv_sems.at[s])
@@ -126,14 +121,18 @@
             src_ref=src, dst_ref=dst, send_sem=send, recv_sem=recv, device_id=partner, device_id_type=MESH
         )
 
-    x_copy = pltpu.make_async_copy(x_ref, x_t, x_sem)
+    x_copies = [
+        pltpu.make_async_copy(src, x_t.at[pl.ds(side * half, half), :], x_sems.at[k])
+        for k, (src, side) in enumerate(((own_ref, tp), (other_ref, 1 - tp)))
+    ]
     small = [
         pltpu.make_async_copy(src, dst, small_sems.at[k])
         for k, (src, dst) in enumerate(
             ((gains_hbm, gains_ref), (segment_hbm, segment_ref), (owner_hbm, owner_ref))
         )
     ]
-    x_copy.start()
+    for copy in x_copies:
+        copy.start()
     for copy in small:
         copy.start()
     for s in range(3):
@@ -155,9 +154,11 @@
         for s in range(3):
             heads[s, h, pl.ds(HEAD_DIM, 128 - HEAD_DIM), :] = jnp.zeros((128 - HEAD_DIM, count), bf16)
     seg_rows = jnp.broadcast_to(segment_ref[...], (count, count))
-    same = seg_rows == seg_rows.T
-
-    x_copy.wait()
+    same = pre_a.at[:, pl.ds(0, count)]
+    same[...] = jnp.where(seg_rows == seg_rows.T, 0.0, -1e30)
+
+    for copy in x_copies:
+        copy.wait()
     total = jnp.zeros((1, count), f32)
     for b in range(width // 128):
         total += jnp.sum(x_t[pl.ds(128 * b, 128), :].astype(f32), axis=0, keepdims=True)
@@ -188,7 +189,7 @@
         scores = lax.dot_general(
             heads[1, h], heads[0, h], (((0,), (0,)), ((), ())), preferred_element_type=f32
         )
-        scores = jnp.where(same, scores * HEAD_DIM ** (-0.5), -1e30)
+        scores = jnp.where(same[...] == 0.0, scores * HEAD_DIM ** (-0.5), -1e30)
         top = jnp.max(scores, axis=0, keepdims=True)
         expo = jnp.exp(scores - top)
         share = 1.0 / jnp.sum(expo, axis=0, keepdims=True)
@@ -241,14 +242,14 @@
         out[...] = (0.5 * u * (1.0 + lax.erf(u * 0.5**0.5))).astype(bf16)
 
     def down(c, hid):
-        acc[...] += jnp.dot(hid[...], down_place(c)[...], preferred_element_type=f32)
+        product = jnp.dot(hid[...], down_place(c)[...], preferred_element_type=f32)
+        acc[...] = product if c == 0 else acc[...] + product
 
     def wait_chunks(chunks):
         for c in chunks:
             up_copy(c).wait()
             down_copy(c).wait()
 
-    acc[...] = jnp.zeros_like(acc)
     wait_chunks(range(middle))
     for m in range(spare):
         merge_copy(m).start()
@@ -350,9 +351,9 @@
     wait_all(sorted_tiles, send_sem_b)
 
 
-def layer(x_t, segment, owner, qkv_t, w_out, w_up, w_down, gains, w_merge):
-    width, count = x_t.shape
-    half = width // 2
+def layer(own, other, segment, owner, qkv_t, w_out, w_up, w_down, gains, w_merge):
+    half, count = own.shape
+    width = 2 * half
     hidden = w_up.shape[1]
     chunk = 512
     chunks = hidden // chunk
@@ -366,7 +367,7 @@
     return pl.pallas_call(
         layer_kernel,
         out_shape=jax.ShapeDtypeStruct((rows, out_width), bf16),
-        in_specs=[hbm] * 9,
+        in_specs=[hbm] * 10,
         out_specs=vmem,
         scratch_shapes=[
             pltpu.VMEM((width, count), bf16),
@@ -397,20 +398,21 @@
             pltpu.VMEM((1, 128), jnp.int32),
             pltpu.SMEM((1, 128), jnp.int32),
         ]
-        + [dma, dma((3,)), dma((3,)), dma((heads,)), dma((slots,)), dma((chunks,))]
+        + [dma((2,)), dma((3,)), dma((3,)), dma((heads,)), dma((slots,)), dma((chunks,))]
         + [dma((3,))] * 4
         + [dma] * 7,
         compiler_params=pltpu.CompilerParams(
             collective_id=2, has_side_effects=True, vmem_limit_bytes=62 * 1024 * 1024
         ),
         name="layer",
-    )(x_t, segment, owner, qkv_t, w_out, w_up, w_down, gains, w_merge)
+    )(own, other, segment, owner, qkv_t, w_out, w_up, w_down, gains, w_merge)
 
 
 def local(patches, segment, owner, w_qkv, w_out, w_up, w_down, gains, w_merge):
-    x_t = swap_halves(patches.T)
+    own = patches.T
     return layer(
-        x_t, segment.reshape(1, -1), owner, w_qkv.transpose(0, 2, 1), w_out, w_up, w_down, gains, w_merge
+        own, swap_halves(own), segment.reshape(1, -1), owner, w_qkv.transpose(0, 2, 1), w_out, w_up, w_down,
+        gains, w_merge,
     )
 
 

time: 53 us -> 52.1 us (0.983)
  Pallas kernels: 51.1 us -> 50.3 us
    pallas_call x1, Pallas kernels: 2.91 us -> 2.13 us  [swap_halves(): pl.pallas_call(swap_kernel, out_shape=jax.ShapeDtypeStruct(patches_t.shap...]
where the time goes in v7:
time: 52.1 us; the launch traced here: 52 us
  Pallas kernels  50.3 us (97%)
  local copies, waits for them, and re-layouts  1.67 us (3%)
    pallas_call x1, Pallas kernels, layer(): pl.pallas_call(layer_kernel, out_shape=jax.ShapeDtypeStruct((rows, out_wi...  48.2 us
    pallas_call x1, Pallas kernels, swap_halves(): pl.pallas_call(swap_kernel, out_shape=jax.ShapeDtypeStruct(patches_t.shap...  2.13 us
    unnamed x1, local copies, waits for them, and re-layouts  1.67 us

profile of v7, /device:TPU:0, one launch (start us, length us, event | category | flops | bytes accessed | tf_op | source)
XLA Modules:
  0.0 52.0 jit_solution(1873531314786301622)
XLA Ops:
  0.0 2.1 %swap_halves.1.other_ref = bf16[832,256]{1,0:T(8,128)(2,1)} custom-call(bf16[832,256]{1,0:T(8,128)(2,1)} %bitcast.4), custom_call_target="tpu_custom_call" | custom-call | tf_op jit(solution)/shard_map/swap_halves/pallas_call | solution.py:50
  2.1 48.2 %layer.1 = bf16[64,2048]{1,0:T(8,128)(2,1)} custom-call(bf16[832,256]{1,0:T(8,128)(2,1)} %bitcast.5, bf16[832,256]{1,0:T(8,128)(2,1)} %swap_halves.1.other_ref, s32[1,256]{1,0:T(1,128)} %bitcast.6, s32[2]{0:T(128)} %owner_hbm.1, bf16[3,832,1664]{2,1,0:T(8,128)(2,1)} %bitcast.3, bf16[832,1664]{1,0:T(8,128)(2,1)} %wout_ref.1, bf16[1664,4096]{1,0:T(8,128)(2,1)} %up_ref.1, ...), custom_call_target="tpu_custom_call" | custom-call | tf_op jit(solution)/shard_map/layer/pallas_call | solution.py:367
  50.3 1.7 %copy.11 = bf16[64,2048]{1,0:T(8,128)(2,1)} copy(bf16[64,2048]{1,0:T(8,128)(2,1)} %layer.1) | data formatting | bytes 524288

commit v8 on v7

--- a/solution.py
+++ b/solution.py
@@ -269,11 +269,13 @@
         down(c + 1, hid_b)
 
     gelu(pre_b, hid_b)
-    down(hidden_chunks - 2, hid_a)
     swaps = []
     for k, (start, size) in enumerate(cuts):
         cols = pl.ds(start, size)
         product = acc[:, cols] + jnp.dot(
+            hid_a[...], down_place(hidden_chunks - 2)[:, cols], preferred_element_type=f32
+        )
+        product += jnp.dot(
             hid_b[...], down_place(hidden_chunks - 1)[:, cols], preferred_element_type=f32
         )
         sent[:, cols] = product.astype(bf16)

time: 52.1 us -> 51.9 us (level)
  no operation moved by 1% of the time
where the time goes in v8:
time: 51.9 us; the launch traced here: 51.8 us
  Pallas kernels  50.1 us (97%)
  local copies, waits for them, and re-layouts  1.67 us (3%)
    pallas_call x1, Pallas kernels, layer(): pl.pallas_call(layer_kernel, out_shape=jax.ShapeDtypeStruct((rows, out_wi...  48 us
    pallas_call x1, Pallas kernels, swap_halves(): pl.pallas_call(swap_kernel, out_shape=jax.ShapeDtypeStruct(patches_t.shap...  2.13 us
    unnamed x1, local copies, waits for them, and re-layouts  1.67 us

profile of v8, /device:TPU:0, one launch (start us, length us, event | category | flops | bytes accessed | tf_op | source)
XLA Modules:
  0.0 51.8 jit_solution(6961608579103093824)
XLA Ops:
  0.0 2.1 %swap_halves.1.other_ref = bf16[832,256]{1,0:T(8,128)(2,1)} custom-call(bf16[832,256]{1,0:T(8,128)(2,1)} %bitcast.4), custom_call_target="tpu_custom_call" | custom-call | tf_op jit(solution)/shard_map/swap_halves/pallas_call | solution.py:50
  2.1 48.0 %layer.1 = bf16[64,2048]{1,0:T(8,128)(2,1)} custom-call(bf16[832,256]{1,0:T(8,128)(2,1)} %bitcast.5, bf16[832,256]{1,0:T(8,128)(2,1)} %swap_halves.1.other_ref, s32[1,256]{1,0:T(1,128)} %bitcast.6, s32[2]{0:T(128)} %owner_hbm.1, bf16[3,832,1664]{2,1,0:T(8,128)(2,1)} %bitcast.3, bf16[832,1664]{1,0:T(8,128)(2,1)} %wout_ref.1, bf16[1664,4096]{1,0:T(8,128)(2,1)} %up_ref.1, ...), custom_call_target="tpu_custom_call" | custom-call | tf_op jit(solution)/shard_map/layer/pallas_call | solution.py:369
  50.1 1.7 %copy.11 = bf16[64,2048]{1,0:T(8,128)(2,1)} copy(bf16[64,2048]{1,0:T(8,128)(2,1)} %layer.1) | data formatting | bytes 524288
